TPU v7x, 32 devices: a whole 2x2x4 slice. The times are simulated.
32 devices in a mesh: dp: 16 (over z, y, x), seq: 2 (over core).
Axes of the slice: x: 2, y: 2, z: 4, core: 2. Of those that a mesh axis runs over, the one named last changes fastest.
Arguments:
- block_in: bfloat16 [16, 256, 768], P('dp', 'seq'), may hold values from -6 to 6
- doc_ids: int32 [16, 256], P('dp', 'seq'), may hold values from 0 to 1, as said below
- positions: int32 [16, 256], P('dp', 'seq'), may hold values from 0 to 223, as said below
- ln1_gain: bfloat16 [768], P(('dp', 'seq')), may hold values from 0.5 to 1.5
- ln1_bias: bfloat16 [768], P(('dp', 'seq')), may hold values from -3 to 3
- qkv_weight: bfloat16 [768, 2304], P(('dp', 'seq')), as said below
- qkv_bias: bfloat16 [2304], P(('dp', 'seq')), may hold values from -3 to 3
- attn_weight: bfloat16 [768, 768], P(('dp', 'seq')), may hold values from -0.875 to 0.875
- attn_bias: bfloat16 [768], P(('dp', 'seq')), may hold values from -3 to 3
- ln2_gain: bfloat16 [768], P(('dp', 'seq')), may hold values from 0.5 to 1.5
- ln2_bias: bfloat16 [768], P(('dp', 'seq')), may hold values from -3 to 3
- fc_weight: bfloat16 [768, 3072], P(('dp', 'seq')), may hold values from -0.21875 to 0.21875
- fc_bias: bfloat16 [3072], P(('dp', 'seq')), may hold values from -3 to 3
- proj_weight: bfloat16 [3072, 768], P(('dp', 'seq')), may hold values from -0.109375 to 0.109375
- proj_bias: bfloat16 [768], P(('dp', 'seq')), may hold values from -3 to 3
- grad_out: bfloat16 [16, 256, 768], P('dp', 'seq'), may hold values from -6 to 6
Outputs:
- block_out: bfloat16 [16, 256, 768], P('dp', 'seq')
- grad_in: bfloat16 [16, 256, 768], P('dp', 'seq')
- grad_ln1_gain: float32 [768], P(('dp', 'seq'))
- grad_ln1_bias: float32 [768], P(('dp', 'seq'))
- grad_qkv_weight: float32 [768, 2304], P(('dp', 'seq'))
- grad_qkv_bias: float32 [2304], P(('dp', 'seq'))
- grad_attn_weight: float32 [768, 768], P(('dp', 'seq'))
- grad_attn_bias: float32 [768], P(('dp', 'seq'))
- grad_ln2_gain: float32 [768], P(('dp', 'seq'))
- grad_ln2_bias: float32 [768], P(('dp', 'seq'))
- grad_fc_weight: float32 [768, 3072], P(('dp', 'seq'))
- grad_fc_bias: float32 [3072], P(('dp', 'seq'))
- grad_proj_weight: float32 [3072, 768], P(('dp', 'seq'))
- grad_proj_bias: float32 [768], P(('dp', 'seq'))
Inputs may be any that keep to these rules, and one draw needn't show every extreme that they name: `doc_ids`: each row holds two documents: id 0 on its first tokens and id 1 on the rest; the first has 32 to 224 tokens. `positions`: each token's index within its document. `qkv_weight`: columns are the query, key and value projections in that order, each with its heads side by side.
All inputs are finite; a program needn't handle non-finite values.
Results may differ from a plain program's by a relative error of at most 0.009.
Values may be sent and summed in bfloat16 or wider, within the bound.
No kernel may reach another device: no remote copies, remote signals or barrier semaphores. Data moves between devices by JAX's collectives and lax.ppermute only.
A program may use at most 192 MiB of HBM per device.

v0:
```python
import math

import jax
import jax.numpy as jnp
from jax import lax
from jax.sharding import PartitionSpec as P

HEADS = 12
HEAD = 64
ROT = 16


EPSILON = 1e-05
ROOT_HALF = 1.0 / math.sqrt(2.0)
ROOT_TWO_PI = 1.0 / math.sqrt(2.0 * math.pi)


def from_behind(shard, axis, by):
    devices = lax.axis_size(axis)
    pairs = [(i, i + by) for i in range(devices) if 0 <= i + by < devices]
    return lax.ppermute(shard, axis, pairs)


def layer_norm(values):
    centred = values - jnp.mean(values, -1, keepdims=True)
    inverse = lax.rsqrt(jnp.mean(centred * centred, -1, keepdims=True) + EPSILON)
    return (centred * inverse, inverse)


def norm_back(upstream, normed, inverse, gain_vec):
    scaled = upstream * gain_vec.astype(jnp.float32)
    return inverse * (
        scaled
        - jnp.mean(scaled, -1, keepdims=True)
        - normed * jnp.mean(scaled * normed, -1, keepdims=True)
    )


def gelu_slope(pre_act):
    return (
        0.5 * (1.0 + lax.erf(pre_act * ROOT_HALF))
        + pre_act * jnp.exp(-0.5 * pre_act * pre_act) * ROOT_TWO_PI
    )


def tables(token_pos):
    half_rot = ROT // 2
    frequency = 10000.0 ** (-(jnp.arange(half_rot).astype(jnp.float32) * 2.0 / ROT))
    angles = token_pos.astype(jnp.float32)[:, None] * frequency[None, :]
    return (jnp.cos(angles)[:, None, :], jnp.sin(angles)[:, None, :])


def rotate(heads, cos_table, sine_table):
    half_rot = ROT // 2
    first = heads[..., :half_rot]
    second = heads[..., half_rot:ROT]
    return jnp.concatenate(
        [
            first * cos_table - second * sine_table,
            second * cos_table + first * sine_table,
            heads[..., ROT:],
        ],
        -1,
    )


def unrotate(heads, cos_table, sine_table):
    half_rot = ROT // 2
    first = heads[..., :half_rot]
    second = heads[..., half_rot:ROT]
    return jnp.concatenate(
        [
            first * cos_table + second * sine_table,
            second * cos_table - first * sine_table,
            heads[..., ROT:],
        ],
        -1,
    )


def local(
    block_in,
    doc_ids,
    positions,
    ln1_gain,
    ln1_bias,
    qkv_weight,
    qkv_bias,
    attn_weight,
    attn_bias,
    ln2_gain,
    ln2_bias,
    fc_weight,
    fc_bias,
    proj_weight,
    proj_bias,
    grad_out,
):
    gathered = (
        lax.all_gather(ln1_gain, ("dp", "seq"), axis=0, tiled=True),
        lax.all_gather(ln1_bias, ("dp", "seq"), axis=0, tiled=True),
        lax.all_gather(qkv_weight, ("dp", "seq"), axis=0, tiled=True),
        lax.all_gather(qkv_bias, ("dp", "seq"), axis=0, tiled=True),
        lax.all_gather(attn_weight, ("dp", "seq"), axis=0, tiled=True),
        lax.all_gather(attn_bias, ("dp", "seq"), axis=0, tiled=True),
        lax.all_gather(ln2_gain, ("dp", "seq"), axis=0, tiled=True),
        lax.all_gather(ln2_bias, ("dp", "seq"), axis=0, tiled=True),
        lax.all_gather(fc_weight, ("dp", "seq"), axis=0, tiled=True),
        lax.all_gather(fc_bias, ("dp", "seq"), axis=0, tiled=True),
        lax.all_gather(proj_weight, ("dp", "seq"), axis=0, tiled=True),
        lax.all_gather(proj_bias, ("dp", "seq"), axis=0, tiled=True),
    )
    (
        norm1_gain,
        norm1_bias,
        qkv_mat,
        qkv_vec,
        out_mat,
        out_vec,
        norm2_gain,
        norm2_bias,
        fc_mat,
        fc_vec,
        proj_mat,
        proj_vec,
    ) = gathered
    row_count, local_len, model_width = block_in.shape
    tokens = row_count * local_len
    offset = lax.axis_index("seq") * local_len
    score_scale = HEAD ** (-0.5)
    float_type = jnp.float32
    inputs = block_in.reshape(tokens, model_width).astype(float_type)
    normed, inverse = layer_norm(inputs)
    acts1 = (normed * norm1_gain.astype(float_type) + norm1_bias.astype(float_type)).astype(
        jnp.bfloat16
    )
    acts2 = (normed * norm2_gain.astype(float_type) + norm2_bias.astype(float_type)).astype(
        jnp.bfloat16
    )
    projected = jnp.dot(acts1, qkv_mat, preferred_element_type=float_type) + qkv_vec.astype(
        float_type
    )
    cos_table, sine_table = tables(positions.reshape(tokens))
    queries = rotate(
        projected[:, :model_width].reshape(tokens, HEADS, HEAD), cos_table, sine_table
    ).astype(jnp.bfloat16)
    keys_own = (
        rotate(
            projected[:, model_width : 2 * model_width].reshape(tokens, HEADS, HEAD),
            cos_table,
            sine_table,
        )
        .astype(jnp.bfloat16)
        .reshape(row_count, local_len, model_width)
    )
    values_own = (
        projected[:, 2 * model_width :]
        .astype(jnp.bfloat16)
        .reshape(row_count, local_len, model_width)
    )
    docs_own = doc_ids.astype(jnp.bfloat16)
    keys_prev, values_prev, docs_prev = from_behind((keys_own, values_own, docs_own), "seq", 1)
    keys_all = jnp.concatenate([keys_prev, keys_own], 1).reshape(
        row_count, 2 * local_len, HEADS, HEAD
    )
    values_all = jnp.concatenate([values_prev, values_own], 1).reshape(
        row_count, 2 * local_len, HEADS, HEAD
    )
    docs_all = jnp.concatenate([docs_prev, docs_own], 1)
    query_heads = queries.reshape(row_count, local_len, HEADS, HEAD)
    query_index = offset + jnp.arange(local_len)
    key_index = offset - local_len + jnp.arange(2 * local_len)
    allowed = (key_index[None, :] <= query_index[:, None]) & (key_index[None, :] >= 0)
    allowed = (allowed[None] & (docs_all[:, None, :] == docs_own[:, :, None]))[:, None]

    def scores_of():
        raw_scores = (
            jnp.einsum("rqhd,rkhd->rhqk", query_heads, keys_all, preferred_element_type=float_type)
            * score_scale
        )
        return jnp.where(allowed, raw_scores, -jnp.inf)

    scores = scores_of()
    row_max = jnp.max(scores, -1, keepdims=True)
    logsum = row_max + jnp.log(jnp.sum(jnp.exp(scores - row_max), -1, keepdims=True))
    probs = jnp.exp(scores - logsum).astype(jnp.bfloat16)
    context = (
        jnp.einsum("rhqk,rkhd->rqhd", probs, values_all, preferred_element_type=float_type)
        .astype(jnp.bfloat16)
        .reshape(tokens, model_width)
    )
    pre_act = jnp.dot(acts2, fc_mat, preferred_element_type=float_type) + fc_vec.astype(float_type)
    hidden = jax.nn.gelu(pre_act, approximate=False).astype(jnp.bfloat16)
    attn_out = jnp.dot(context, out_mat, preferred_element_type=float_type) + out_vec.astype(
        float_type
    )
    mlp_out = jnp.dot(hidden, proj_mat, preferred_element_type=float_type) + proj_vec.astype(
        float_type
    )
    block_out = (
        (inputs + attn_out + mlp_out)
        .astype(jnp.bfloat16)
        .reshape(row_count, local_len, model_width)
    )
    (
        norm1_gain,
        norm1_bias,
        qkv_mat,
        qkv_vec,
        out_mat,
        out_vec,
        norm2_gain,
        norm2_bias,
        fc_mat,
        fc_vec,
        proj_mat,
        proj_vec,
    ) = gathered
    upstream_b = grad_out.reshape(tokens, model_width)
    upstream = upstream_b.astype(float_type)
    grad_proj_bias = jnp.sum(upstream, 0)
    grad_proj_weight = jnp.einsum(
        "nf,nd->fd", hidden, upstream_b, preferred_element_type=float_type
    )
    d_pre = jnp.einsum(
        "nd,fd->nf", upstream_b, proj_mat, preferred_element_type=float_type
    ) * gelu_slope(pre_act)
    grad_fc_bias = jnp.sum(d_pre, 0)
    d_pre_b = d_pre.astype(jnp.bfloat16)
    grad_fc_weight = jnp.einsum("nd,nf->df", acts2, d_pre_b, preferred_element_type=float_type)
    d_acts2 = jnp.einsum("nf,df->nd", d_pre_b, fc_mat, preferred_element_type=float_type)
    grad_ln2_gain = jnp.sum(d_acts2 * normed, 0)
    grad_ln2_bias = jnp.sum(d_acts2, 0)
    grad_attn_bias = jnp.sum(upstream, 0)
    grad_attn_weight = jnp.einsum(
        "nc,nd->cd", context, upstream_b, preferred_element_type=float_type
    )
    d_context = jnp.einsum(
        "nd,cd->nc", upstream_b, out_mat, preferred_element_type=float_type
    ).astype(jnp.bfloat16)
    d_ctx_heads = d_context.reshape(row_count, local_len, HEADS, HEAD)
    row_dot = jnp.sum(
        d_ctx_heads.astype(float_type)
        * context.reshape(row_count, local_len, HEADS, HEAD).astype(float_type),
        -1,
    )
    scores = scores_of()
    weights_full = jnp.exp(scores - logsum)
    d_weights = jnp.einsum(
        "rqhd,rkhd->rhqk", d_ctx_heads, values_all, preferred_element_type=float_type
    )
    d_scores = (
        weights_full * (d_weights - jnp.transpose(row_dot, (0, 2, 1))[..., None]) * score_scale
    ).astype(jnp.bfloat16)
    d_query = jnp.einsum("rhqk,rkhd->rqhd", d_scores, keys_all, preferred_element_type=float_type)
    d_keys = jnp.einsum(
        "rhqk,rqhd->rkhd", d_scores, query_heads, preferred_element_type=float_type
    ).reshape(row_count, 2 * local_len, model_width)
    d_values = jnp.einsum(
        "rhqk,rqhd->rkhd", probs, d_ctx_heads, preferred_element_type=float_type
    ).reshape(row_count, 2 * local_len, model_width)
    back_keys, back_values = (
        from_behind(d_keys[:, :local_len].astype(jnp.bfloat16), "seq", -1).astype(jnp.float32),
        from_behind(d_values[:, :local_len].astype(jnp.bfloat16), "seq", -1).astype(jnp.float32),
    )
    d_keys_own = (d_keys[:, local_len:] + back_keys).reshape(tokens, HEADS, HEAD)
    d_values_own = (d_values[:, local_len:] + back_values).reshape(tokens, model_width)
    d_projected = jnp.concatenate(
        [
            unrotate(d_query.reshape(tokens, HEADS, HEAD), cos_table, sine_table).reshape(
                tokens, model_width
            ),
            unrotate(d_keys_own, cos_table, sine_table).reshape(tokens, model_width),
            d_values_own,
        ],
        1,
    )
    grad_qkv_bias = jnp.sum(d_projected, 0)
    d_proj_b = d_projected.astype(jnp.bfloat16)
    grad_qkv_weight = jnp.einsum("nd,ne->de", acts1, d_proj_b, preferred_element_type=float_type)
    d_acts1 = jnp.einsum("ne,de->nd", d_proj_b, qkv_mat, preferred_element_type=float_type)
    grad_ln1_gain = jnp.sum(d_acts1 * normed, 0)
    grad_ln1_bias = jnp.sum(d_acts1, 0)
    grad_in = (
        (
            upstream
            + norm_back(d_acts1, normed, inverse, norm1_gain)
            + norm_back(d_acts2, normed, inverse, norm2_gain)
        )
        .astype(jnp.bfloat16)
        .reshape(row_count, local_len, model_width)
    )
    summed = (
        lax.psum_scatter(grad_ln1_gain, ("dp", "seq"), scatter_dimension=0, tiled=True),
        lax.psum_scatter(grad_ln1_bias, ("dp", "seq"), scatter_dimension=0, tiled=True),
        lax.psum_scatter(grad_qkv_weight, ("dp", "seq"), scatter_dimension=0, tiled=True),
        lax.psum_scatter(grad_qkv_bias, ("dp", "seq"), scatter_dimension=0, tiled=True),
        lax.psum_scatter(grad_attn_weight, ("dp", "seq"), scatter_dimension=0, tiled=True),
        lax.psum_scatter(grad_attn_bias, ("dp", "seq"), scatter_dimension=0, tiled=True),
        lax.psum_scatter(grad_ln2_gain, ("dp", "seq"), scatter_dimension=0, tiled=True),
        lax.psum_scatter(grad_ln2_bias, ("dp", "seq"), scatter_dimension=0, tiled=True),
        lax.psum_scatter(grad_fc_weight, ("dp", "seq"), scatter_dimension=0, tiled=True),
        lax.psum_scatter(grad_fc_bias, ("dp", "seq"), scatter_dimension=0, tiled=True),
        lax.psum_scatter(grad_proj_weight, ("dp", "seq"), scatter_dimension=0, tiled=True),
        lax.psum_scatter(grad_proj_bias, ("dp", "seq"), scatter_dimension=0, tiled=True),
    )
    return (
        block_out,
        grad_in,
        summed[0],
        summed[1],
        summed[2],
        summed[3],
        summed[4],
        summed[5],
        summed[6],
        summed[7],
        summed[8],
        summed[9],
        summed[10],
        summed[11],
    )


def solution(mesh):
    placed = (
        P("dp", "seq", None),
        P("dp", "seq"),
        P("dp", "seq"),
        P(("dp", "seq")),
        P(("dp", "seq")),
        P(("dp", "seq"), None),
        P(("dp", "seq")),
        P(("dp", "seq"), None),
        P(("dp", "seq")),
        P(("dp", "seq")),
        P(("dp", "seq")),
        P(("dp", "seq"), None),
        P(("dp", "seq")),
        P(("dp", "seq"), None),
        P(("dp", "seq")),
        P("dp", "seq", None),
    )
    return jax.shard_map(
        local,
        mesh=mesh,
        in_specs=placed,
        out_specs=(
            P("dp", "seq", None),
            P("dp", "seq", None),
            P(("dp", "seq")),
            P(("dp", "seq")),
            P(("dp", "seq"), None),
            P(("dp", "seq")),
            P(("dp", "seq"), None),
            P(("dp", "seq")),
            P(("dp", "seq")),
            P(("dp", "seq")),
            P(("dp", "seq"), None),
            P(("dp", "seq")),
            P(("dp", "seq"), None),
            P(("dp", "seq")),
        ),
        check_vma=False,
    )
```

profile of v0, /device:TPU:0, one launch (start us, length us, event | category | flops | bytes accessed | tf_op | source)
XLA Modules:
  0.0 778.8 jit_solution(5045780520184419339)
XLA Ops:
  7.2 0.7 all-gather.7.cloned.1.call-update
  8.0 0.7 all-gather.5.cloned.1.call-update
  8.7 0.7 all-gather.9.cloned.1.call-update
  10.7 2.4 collective-permute-start.1
  13.1 0.8 dynamic-update-slice
  14.0 0.8 dynamic-update-slice.1
  14.8 0.8 dynamic-update-slice.7
  15.6 0.8 dynamic-update-slice.4
  16.5 0.8 dynamic-update-slice.5
  17.3 0.8 dynamic-update-slice.3
  18.1 0.8 dynamic-update-slice.2
  19.0 0.8 dynamic-update-slice.6
  19.8 42.1 %all-reduce.16 = (bf16[3072]{0:T(1024)(128)(2,1)}, bf16[768]{0:T(1024)(128)(2,1)}, bf16[768]{0:T(1024)(128)(2,1)}, bf16[768]{0:T(1024)(128)(2,1)}, bf16[2304]{0:...) all-reduce(bf16[3072]{0:T(1024)(128)(2,1)S(1)} %dynamic-update-slic, ...), channel_id=1, replica_groups=mesh['dp'=16,'seq'=2] {'dp','seq'}, use_global_device_ids=true, to_apply=%add.6 | all-reduce | flops 9984 | bytes 39936
  62.0 1.0 convert_reduce_fusion.1
  63.0 1.1 fusion.46
  64.1 0.7 convert_bitcast_fusion.1
  65.0 0.7 compare_and_fusion
  65.7 2.0 all-gather.7.cloned.1.call-done
  67.8 1.9 convolution_convert_fusion
  69.8 59.9 %all-gather.5.cloned.1.call-done = bf16[768,2304]{1,0:T(8,128)(2,1)} async-done(((bf16[24,2304]{1,0:T(8,128)(2,1)}), bf16[768,2304]{1,0:T(8,128)(2,1)}) %all-gather.5.cloned.1.call-update) | async-done | bytes 3538960 | tf_op jit(solution)/shard_map/all_gather | solution.py:102
  129.7 2.7 convolution_add_fusion
  132.9 2.2 collective-permute-start
  135.4 1.3 collective-permute-start.2
  136.9 0.8 collective-permute-done.2
  137.8 1.3 fusion.77
  139.6 1.1 multiply_reduce_fusion
  140.7 1.8 fusion.57
  143.2 0.7 multiply_convert_fusion
  144.8 1.3 collective-permute-start.4
  146.1 1.3 collective-permute-start.3
  147.9 1.6 collective-permute-done.3
  150.2 4.1 fusion.68
  155.0 40.0 %all-gather.9.cloned.1.call-done = bf16[768,3072]{1,0:T(8,128)(2,1)} async-done(((bf16[24,3072]{1,0:T(8,128)(2,1)}), bf16[768,3072]{1,0:T(8,128)(2,1)}) %all-gather.9.cloned.1.call-update) | async-done | bytes 4718608 | tf_op jit(solution)/shard_map/all_gather | solution.py:108
  195.1 7.6 fusion.2
  202.7 57.1 %all-gather.11.cloned.1.call-done = bf16[3072,768]{1,0:T(8,128)(2,1)} async-done(((bf16[96,768]{1,0:T(8,128)(2,1)}), bf16[3072,768]{1,0:T(8,128)(2,1)}) %all-gather.11.cloned.1.call-update) | async-done | bytes 4718608 | tf_op jit(solution)/shard_map/all_gather | solution.py:110
  259.8 4.6 fusion.78
  264.4 5.1 fusion.48
  269.6 5.1 fusion.55
  275.7 4.2 fusion.50
  279.9 1.5 fusion.44
  281.5 1.0 convert_reduce_fusion
  282.5 40.1 %all-reduce.15 = (f32[768]{0:T(1024)S(1)}, f32[768]{0:T(1024)S(1)}, f32[2304]{0:T(1024)S(1)}, f32[768]{0:T(1024)S(1)}, f32[768]{0:T(1024)S(1)}, /*index=5*/f32[768]{0:T(1024)S(1)}, f32[3072]{0:T(1024)S(1)}) all-reduce(f32[768]{0:T(1024)S(1)} %get-tuple-element.16, ...), channel_id=2, replica_groups=mesh['dp'=16,'seq'=2] {'dp','seq'}, use_global_device_ids=true, to_apply=%region_10.11.clone | all-reduce | flops 9216 | bytes 73728
  326.2 3.2 convolution_add_fusion.3
  329.5 1.0 fusion.18
  330.6 32.9 %reduce-scatter.7.cloned.1.call-done = f32[24,768]{1,0:T(8,128)} async-done(((f32[768,768]{1,0:T(8,128)}), f32[24,768]{1,0:T(8,128)}) %reduce-scatter.7.cloned.1.call-update) | async-done | bytes 73744 | tf_op jit(solution)/shard_map/reduce_scatter | solution.py:298
  363.5 124.8 %reduce-scatter.5.cloned.1.call-done = f32[24,2304]{1,0:T(8,128)} async-done(((f32[768,2304]{1,0:T(8,128)}), f32[24,2304]{1,0:T(8,128)}) %reduce-scatter.5.cloned.1.call-update) | async-done | bytes 221200 | tf_op jit(solution)/shard_map/reduce_scatter | solution.py:296
  488.3 141.6 %reduce-scatter.9.cloned.1.call-done = f32[24,3072]{1,0:T(8,128)} async-done(((f32[768,3072]{1,0:T(8,128)}), f32[24,3072]{1,0:T(8,128)}) %reduce-scatter.9.cloned.1.call-update) | async-done | bytes 294928 | tf_op jit(solution)/shard_map/reduce_scatter | solution.py:302
  629.9 141.6 %reduce-scatter.11.cloned.1.call-done = f32[96,768]{1,0:T(8,128)} async-done(((f32[3072,768]{1,0:T(8,128)}), f32[96,768]{1,0:T(8,128)}) %reduce-scatter.11.cloned.1.call-update) | async-done | bytes 294928 | tf_op jit(solution)/shard_map/reduce_scatter | solution.py:304
  (135 shorter events, 11.6 us)
Async XLA Ops:
  7.2 60.6 %all-gather.7.cloned.1.call-start = ((), (), s32[]{:S(2)}) async-start(), calls=%async_computation.5 | async-start | bytes 1216512 | tf_op jit(solution)/shard_map/all_gather | solution.py:104
  7.9 121.8 %copy-start = (bf16[1,128,768]{2,1,0:T(8,128)(2,1)S(1)}, bf16[1,128,768]{2,1,0:T(8,128)(2,1)}, u32[]{:S(2)}) copy-start(bf16[1,128,768]{2,1,0:T(8,128)(2,1)} %param.16) | copy-start | bytes 589828
  7.9 121.8 %all-gather.5.cloned.1.call-start = ((), (), s32[]{:S(2)}) async-start(), calls=%async_computation.4 | async-start | bytes 3649536 | tf_op jit(solution)/shard_map/all_gather | solution.py:102
  8.7 186.4 %all-gather.9.cloned.1.call-start = ((), (), s32[]{:S(2)}) async-start(), calls=%async_computation.6 | async-start | bytes 4866048 | tf_op jit(solution)/shard_map/all_gather | solution.py:108
  9.4 250.4 %all-gather.11.cloned.1.call-start = ((), (), s32[]{:S(2)}) async-start(), calls=%async_computation.7 | async-start | bytes 4866048 | tf_op jit(solution)/shard_map/all_gather | solution.py:110
  10.0 353.5 %reduce-scatter.7.cloned.1.call-start = ((), (), s32[]{:S(2)}) async-start(), calls=%async_computation.9 | async-start | bytes 2433024 | tf_op jit(solution)/shard_map/reduce_scatter | solution.py:298
  10.7 54.3 %collective-permute-start.1 = (bf16[1,128]{1,0:T(2,128)(2,1)S(1)}, bf16[1,128]{1,0:T(2,128)(2,1)S(1)}, u32[]{:S(2)}, u32[]{:S(2)}) collective-permute-start(bf16[1,128]{1,0:T(2,128)(2,1)S(1)} %get-tuple-element.60), channel_id=1, source_target_pairs={{0,1},{2,3},{4,5},{6,7},{8,9},{10,11},{12,13},{14,15},{16,17},{18,... | collective-permute-start | bytes 776 | tf_op jit(solution)/shard_map/ppermute | solution.py:21
  63.0 66.7 %copy-start.15 = (f32[128]{0:T(128)}, f32[128]{0:T(128)S(1)}, u32[]{:S(2)}) copy-start(f32[128]{0:T(128)S(1)} %broadcast_multiply_fusion.4) | copy-start | bytes 1540
  64.8 64.9 %copy-start.17 = (f32[128]{0:T(128)}, f32[128]{0:T(128)S(1)}, u32[]{:S(2)}) copy-start(f32[128]{0:T(128)S(1)} %add_rsqrt_fusion) | copy-start | bytes 1540
  64.9 70.4 %copy-start.10 = (f32[128,8]{0,1:T(8,128)}, f32[128,8]{0,1:T(8,128)S(1)}, u32[]{:S(2)}) copy-start(f32[128,8]{0,1:T(8,128)S(1)} %get-tuple-element.57) | copy-start | bytes 12292
  64.9 70.4 %copy-start.12 = (f32[128,8]{0,1:T(8,128)}, f32[128,8]{0,1:T(8,128)S(1)}, u32[]{:S(2)}) copy-start(f32[128,8]{0,1:T(8,128)S(1)} %get-tuple-element.58) | copy-start | bytes 12292
  132.9 3.8 collective-permute-start
  135.3 3.7 copy-start.6
  135.4 3.7 copy-start.8
  135.4 2.4 collective-permute-start.2
  136.7 2.3 copy-start.4
  137.8 1.3 copy-start.24
  139.6 1.1 copy-start.3
  142.5 0.7 copy-start.14
  142.6 345.8 %reduce-scatter.5.cloned.1.call-start = ((), (), s32[]{:S(2)}) async-start(), calls=%async_computation.8 | async-start | bytes 7299072 | tf_op jit(solution)/shard_map/reduce_scatter | solution.py:296
  144.2 3.2 copy-start.5
  144.2 3.2 copy-start.7
  144.2 3.2 copy-start.9
  144.2 3.2 copy-start.25
  144.8 4.7 copy-start.11
  144.8 4.7 copy-start.13
  144.8 4.9 collective-permute-start.4
  146.1 3.3 collective-permute-start.3
  149.5 0.7 copy-start.16
  149.5 0.7 copy-start.18
  154.3 0.7 copy-start.23
  154.3 0.7 copy-start.22
  154.3 0.7 copy-start.19
  154.4 475.5 %reduce-scatter.9.cloned.1.call-start = ((), (), s32[]{:S(2)}) async-start(), calls=%async_computation.10 | async-start | bytes 9732096 | tf_op jit(solution)/shard_map/reduce_scatter | solution.py:302
  269.5 502.0 %reduce-scatter.11.cloned.1.call-start = ((), (), s32[]{:S(2)}) async-start(), calls=%async_computation.11 | async-start | bytes 9732096 | tf_op jit(solution)/shard_map/reduce_scatter | solution.py:304
  274.6 0.7 copy-start.21
  274.6 0.7 copy-start.20
  275.7 4.2 copy-start.2
  323.3 448.2 %copy-start.26 = (f32[24]{0:T(128)}, f32[24]{0:T(128)S(1)}, u32[]{:S(2)}) copy-start(f32[24]{0:T(128)S(1)} %dynamic-slice.3) | copy-start | bytes 292
  326.2 3.2 copy-start.1
Sparse Core Ops, SparseCore 0:
  10.9 56.8 all-gather.6
  70.7 59.0 all-gather.4
  132.6 62.3 all-gather.8
  197.8 61.9 all-gather.10
  265.5 97.9 reduce-scatter.6
  369.6 118.6 reduce-scatter.4
  494.8 135.0 reduce-scatter.8
  636.3 135.1 reduce-scatter.10
where the time goes:
time: 780 us; the launch traced here: 779 us
  waiting for transfers between devices  605 us (78%)
  blocking collectives  82.2 us (11%)
  matrix products  47.1 us (6%)
  between operations  14.8 us (2%)
  local copies, waits for them, and re-layouts  14.1 us (2%)
  starting transfers between devices  8.92 us (1%)
    reduce_scatter x1, waiting for transfers between devices, local(): lax.psum_scatter(grad_proj_weight, ('dp', 'seq'), scatter_dimension=0, ti...  142 us
    reduce_scatter x1, waiting for transfers between devices, local(): lax.psum_scatter(grad_fc_weight, ('dp', 'seq'), scatter_dimension=0, tile...  142 us
    reduce_scatter x1, waiting for transfers between devices, local(): lax.psum_scatter(grad_qkv_weight, ('dp', 'seq'), scatter_dimension=0, til...  125 us
    unnamed x2, blocking collectives  82.2 us
    all_gather x1, waiting for transfers between devices, local(): lax.all_gather(qkv_weight, ('dp', 'seq'), axis=0, tiled=True)  59.9 us
    all_gather x1, waiting for transfers between devices, local(): lax.all_gather(proj_weight, ('dp', 'seq'), axis=0, tiled=True)  57.1 us
    all_gather x1, waiting for transfers between devices, local(): lax.all_gather(fc_weight, ('dp', 'seq'), axis=0, tiled=True)  40 us
    reduce_scatter x1, waiting for transfers between devices, local(): lax.psum_scatter(grad_attn_weight, ('dp', 'seq'), scatter_dimension=0, ti...  32.9 us
  transfers between devices with their start and end apart: 13, of which 10 were waited for; matrix products, arithmetic and copies ran while one was open for 8% of the time, Pallas kernels for 0%

commit v1 on v0

v1 whole, which is shorter than its diff:
```python
import functools
import math

import jax
import jax.numpy as jnp
from jax import lax
from jax.experimental import pallas as pl
from jax.experimental.pallas import tpu as pltpu
from jax.sharding import Mesh, PartitionSpec as P


HEADS = 12
HEAD = 64
ROT = 16

EPSILON = 1e-05
ROOT_HALF = 1.0 / math.sqrt(2.0)
ROOT_TWO_PI = 1.0 / math.sqrt(2.0 * math.pi)

F32 = jnp.float32
BF16 = jnp.bfloat16


def shifted(value, axis, by):
    count = lax.axis_size(axis)
    return lax.ppermute(value, axis, [(i, (i - by) % count) for i in range(count)])


def exchange(blocks, axis):
    return lax.all_to_all(blocks, axis, 0, 0)


def after(value, *others):
    return lax.optimization_barrier((value,) + others)[0]


def swapped(value):
    cores = lax.axis_size("c")
    return lax.ppermute(value, "c", [(i, cores - 1 - i) for i in range(cores)])


def around(value):
    ranks = lax.axis_size("r")
    mine = [value] + [shifted(value, "r", by) for by in range(1, ranks)]
    return mine, [swapped(block) for block in mine]


def in_order(mine, other):
    first = lax.axis_index("c") == 0
    mine, other = jnp.stack(mine), jnp.stack(other)
    both = jnp.stack([jnp.where(first, mine, other), jnp.where(first, other, mine)], 1)
    return jnp.roll(both, lax.axis_index("r"), 0)


def order_body(ranks, split, place_ref, *refs):
    blocks, outs = refs[: 2 * ranks], refs[2 * ranks :]
    core, rank = place_ref[0], place_ref[1]
    for by in range(ranks):
        spot = lax.rem(rank + by, ranks)
        for (start, count), out in zip(split, outs):
            mine = blocks[by][..., start : start + count, :].astype(F32)
            other = blocks[ranks + by][..., start : start + count, :].astype(F32)
            low = jnp.where(core == 0, mine, other)
            high = jnp.where(core == 0, other, mine)
            pair = jnp.concatenate([low, high], -2).astype(BF16)
            rows = pl.ds(pl.multiple_of(spot * 2 * count, 16), 2 * count)
            if pair.ndim == 2:
                out[rows, :] = pair
            else:
                for i in range(pair.shape[0]):
                    out[i, rows, :] = pair[i]


def pair_summed(blocks, axis):
    core = lax.axis_index("c")
    kept = lax.dynamic_index_in_dim(blocks, core, axis, keepdims=False)
    given = lax.dynamic_index_in_dim(blocks, 1 - core, axis, keepdims=False)
    return kept + swapped(given.astype(BF16)).astype(F32)


def summed(blocks, axis):
    count = lax.axis_size(axis)
    if count > MOST:
        return jnp.sum(exchange(blocks, axis).astype(F32), 0)
    spot = lax.axis_index(axis)
    total = lax.dynamic_index_in_dim(blocks, spot, 0, keepdims=False).astype(F32)
    for by in range(1, count):
        given = lax.dynamic_index_in_dim(blocks, (spot + by) % count, 0, keepdims=False)
        total = total + shifted(given, axis, -by).astype(F32)
    return total


def times(left, right, contract):
    return lax.dot_general(left, right, ((contract[:1], contract[1:]), ((), ())),
                           preferred_element_type=F32)


def kernel_call(body, outs, flops, scratch=(), scalars=0):
    def run(*operands):
        moved = sum(math.prod(a.shape) * a.dtype.itemsize for a in (*operands, *outs))
        return pl.pallas_call(
            body,
            out_shape=outs,
            in_specs=[pl.BlockSpec(memory_space=pltpu.SMEM)] * scalars
            + [pl.BlockSpec(memory_space=pltpu.VMEM)] * (len(operands) - scalars),
            out_specs=tuple(pl.BlockSpec(memory_space=pltpu.VMEM) for _ in outs),
            scratch_shapes=scratch,
            cost_estimate=pl.CostEstimate(flops=flops, bytes_accessed=moved, transcendentals=0),
        )(*operands)

    return run


def shape(*dims, dtype=F32):
    return jax.ShapeDtypeStruct(dims, dtype)


def pack_body(lines, part, units, count, qkv_ref, fc_ref, small_ref, out_ref):
    third = lines * part
    share = qkv_ref.shape[0]
    small = small_ref[...].astype(F32)
    lane = lax.broadcasted_iota(jnp.int32, (share, small.shape[1]), 1)
    row = lax.broadcasted_iota(jnp.int32, (share, small.shape[1]), 0)
    column = lax.broadcasted_iota(jnp.int32, (share, LANES), 1)
    table = jnp.zeros((share, LANES), F32)
    for j in range(count):
        chosen = jnp.where(lane == row + j * share, small, 0.0)
        table = jnp.where(column == j, jnp.sum(chosen, 1, keepdims=True), table)
    for i in range(lines):
        for kind in range(3):
            start = kind * third + i * part
            out_ref[i, :, kind * part : (kind + 1) * part] = qkv_ref[:, start : start + part]
        out_ref[i, :, 3 * part : 3 * part + units] = fc_ref[:, i * units : (i + 1) * units]
        out_ref[i, :, 3 * part + units :] = table.astype(BF16)


def picked(table, at, row, first):
    depth, width = table.shape[1], at.shape[1]
    chosen = lax.broadcasted_iota(jnp.int32, (depth, width), 0) == at
    values = times(table.astype(BF16), chosen.astype(F32).astype(BF16), (1, 0))
    here = lax.broadcasted_iota(jnp.int32, values.shape, 0) == row + first
    return jnp.sum(jnp.where(here, values, 0.0), 0, keepdims=True)


def turned(chunk, cos_table, sine_table):
    lane = lax.broadcasted_iota(jnp.int32, chunk.shape, 1) % HEAD
    width = chunk.shape[1]
    other = jnp.where(
        lane < ROT // 2, pltpu.roll(chunk, width - ROT // 2, 1), pltpu.roll(chunk, ROT // 2, 1)
    )
    return chunk * cos_table + other * sine_table


LANES = 128
MOST = 4


def project_body(own, part, pieces, x_refs, rest):
    (weights_ref, at_q_ref, row_q_ref, at_f_ref, row_f_ref, frequency_ref,
     qkv_ref, acts1_ref, acts2_ref, normed_ref, cos_ref, sine_ref, place_ref, vectors_ref) = rest
    columns = weights_ref.shape[1]
    table = weights_ref[:, columns - LANES :].astype(F32).T
    qkv_vec = picked(table[:16], at_q_ref[...], row_q_ref[...], 6)
    fc_vec = picked(table[:16], at_f_ref[...], row_f_ref[...], 9)
    vectors_ref[0:6] = table[0:6]
    vectors_ref[6:7] = fc_vec
    for i in range(pieces):
        rows = slice(i * own, (i + 1) * own)
        x = x_refs[i][0:own].astype(F32)
        centred = x - jnp.mean(x, -1, keepdims=True)
        normed = centred * lax.rsqrt(jnp.mean(centred * centred, -1, keepdims=True) + EPSILON)
        normed_ref[rows] = normed
        acts1_ref[rows] = (normed * table[0:1] + table[1:2]).astype(BF16)
        acts2_ref[rows] = (normed * table[2:3] + table[3:4]).astype(BF16)
        place = x_refs[i][own : own + 8, 0:own].astype(F32)[0:1]
        angle = frequency_ref[...] * place
        cosine, sine = jnp.cos(angle), jnp.sin(angle)
        ones = jnp.ones((HEAD - ROT, own), F32)
        cos_head = [cosine, cosine, ones]
        sine_head = [-sine, sine, ones * 0.0]
        cos_ref[rows] = jnp.concatenate(cos_head * (LANES // HEAD), 0).T
        sine_ref[rows] = jnp.concatenate(sine_head * (LANES // HEAD), 0).T
        place_ref[rows] = jnp.broadcast_to(place, (LANES, own)).T
    projected = times(acts1_ref[...], weights_ref[:, : 3 * part], (1, 0)) + qkv_vec
    for start in range(0, 2 * part, LANES):
        lanes = slice(start, start + LANES)
        qkv_ref[:, lanes] = turned(projected[:, lanes], cos_ref[...], sine_ref[...]).astype(BF16)
    qkv_ref[:, 2 * part :] = projected[:, 2 * part :].astype(BF16)


def hidden_body(part, acts2_ref, weights_ref, proj_ref, vectors_ref, hidden_ref, slope_ref, out_ref):
    units = proj_ref.shape[0]
    pre_act = times(acts2_ref[...], weights_ref[:, 3 * part : 3 * part + units], (1, 0))
    pre_act = pre_act + vectors_ref[6:7]
    below = 0.5 * (1.0 + lax.erf(pre_act * ROOT_HALF))
    hidden_ref[...] = (pre_act * below).astype(BF16)
    slope_ref[...] = below + pre_act * jnp.exp(-0.5 * pre_act * pre_act) * ROOT_TWO_PI
    out_ref[...] = times(hidden_ref[...], proj_ref[...], (1, 0))


def both_halves(prev_ref, own_ref, i, start):
    lanes = slice(start, start + HEAD)
    return jnp.concatenate([prev_ref[i, :, lanes], own_ref[i, :, lanes]], 0)


def attend_body(own, heads, qkv_ref, prev_ref, place_ref, mat_ref, mlp_ref,
                probs_ref, context_ref, first_ref, *rest):
    part = heads * HEAD
    pieces, out_ref = rest[:-1], rest[-1]
    key = lax.broadcasted_iota(jnp.int32, (own, 2 * own), 1) - own
    query = lax.broadcasted_iota(jnp.int32, (own, 2 * own), 0)

    @pl.loop(0, qkv_ref.shape[0])
    def _(i):
        place = jnp.broadcast_to(place_ref[i][:, 0:1], (own, 2 * own)).astype(jnp.int32)
        allowed = (key <= query) & (key >= query - place)
        for head in range(heads):
            start = head * HEAD
            keys = both_halves(prev_ref, qkv_ref, i, part + start)
            values = both_halves(prev_ref, qkv_ref, i, 2 * part + start)
            scores = times(qkv_ref[i, :, start : start + HEAD], keys, (1, 1)) * HEAD ** (-0.5)
            scores = jnp.where(allowed, scores, -jnp.inf)
            top = jnp.max(scores, -1, keepdims=True)
            logsum = top + jnp.log(jnp.sum(jnp.exp(scores - top), -1, keepdims=True))
            weights = jnp.exp(scores - logsum)
            probs_ref[i, head] = weights
            context_ref[i, :, start : start + HEAD] = times(
                weights.astype(BF16), values, (1, 0)
            ).astype(BF16)
        total = times(context_ref[i], mat_ref[...], (1, 0)) + mlp_ref[i]
        out_ref[i] = total.astype(BF16)

        @pl.when(i == 0)
        def _():
            first_ref[...] = total

    for i, piece in enumerate(pieces):
        piece[...] = out_ref[i + 1]


def dealt(core, values, kept_ref, given_ref, i, row, start, count):
    low = values[start : start + count]
    high = values[start + count : start + 2 * count]
    rows = slice(row, row + count)
    kept_ref[i, rows] = jnp.where(core == 0, low, high)
    given_ref[i, rows] = jnp.where(core == 0, high, low).astype(BF16)


def halves(values):
    high = values.astype(BF16).astype(F32)
    return high, values - high


def hidden_back_body(part, lines, own, dims, *refs):
    place_ref, refs = refs[0], refs[1:]
    (hidden_ref, slope_ref, acts2_ref, weights_ref, proj_ref, vectors_ref, normed_ref, context_ref,
     sums_ref, e_ref, grad_ref, *rest) = refs[lines:]
    if dims:
        kept_ref, given_ref, grad_proj_ref, grad_fc_ref, grad_mat_ref, unit_ref = rest
    else:
        grad_proj_ref, grad_fc_ref, grad_mat_ref, unit_ref = rest
    units = proj_ref.shape[0]
    for i in range(lines):
        grad_ref[i * own : (i + 1) * own] = refs[i][...]
    grad = grad_ref[...]
    grad_mat_ref[...] = times(context_ref[...], grad, (0, 0))
    d_pre = times(grad, proj_ref[...], (1, 1)) * slope_ref[...]
    unit_ref[0:1] = jnp.sum(d_pre, 0, keepdims=True)
    d_pre = d_pre.astype(BF16)
    grad_proj_ref[...] = times(hidden_ref[...], grad, (0, 0))
    grad_fc_ref[...] = times(acts2_ref[...], d_pre, (0, 0))
    d_acts2 = times(d_pre, weights_ref[:, 3 * part : 3 * part + units], (1, 1))
    sums_ref[0:1] = jnp.sum(d_acts2 * normed_ref[...], 0, keepdims=True)
    sums_ref[1:2] = jnp.sum(d_acts2, 0, keepdims=True)
    sums_ref[2:3] = jnp.sum(refs[0][...].astype(F32), 0, keepdims=True)
    e_ref[...] = d_acts2 * vectors_ref[2:3]
    if dims:
        ranks, share, hidden_share = dims
        core = place_ref[0]
        row = lax.broadcasted_iota(jnp.int32, (8, units), 0)
        unit = jnp.broadcast_to(unit_ref[0:1], (8, units))
        high, low = halves(unit)
        base = hidden_share + share
        for i in range(ranks):
            dealt(core, grad_proj_ref, kept_ref, given_ref, i, 0, 2 * i * hidden_share,
                  hidden_share)
            dealt(core, grad_mat_ref, kept_ref, given_ref, i, hidden_share, 2 * i * share, share)
            kept_ref[i, base : base + 8] = jnp.where(row == 0, unit, 0.0)
            given_ref[i, base : base + 8] = jnp.where(
                row == 0, high, jnp.where(row == 1, low, 0.0)
            ).astype(BF16)
            for j in range(lines):
                dealt(core, grad_fc_ref, kept_ref, given_ref, i, base + 8 + j * share,
                      (j * ranks + i) * 2 * share, share)


def fold_body(ranks, start, step, place_ref, kept_ref, got_ref, own_ref, *sent):
    rank = place_ref[1]
    for by in range(ranks):
        spot = lax.rem(rank + by, ranks)
        total = kept_ref[spot] + got_ref[spot].astype(F32)
        if by == 0:
            own_ref[...] = total
        else:
            sent[by - 1][...] = total.astype(BF16)
            if step == 1:
                value = total[start : start + 8]
                value = value[0:1] + value[1:2]
                row = lax.broadcasted_iota(jnp.int32, (8, value.shape[1]), 0)
                high, low = halves(jnp.broadcast_to(value, row.shape))
                value = jnp.where(row == 0, high, jnp.where(row == 1, low, 0.0))
                sent[by - 1][start : start + 8] = value.astype(BF16)
            else:
                value = total[start : start + step] + total[start + step : start + 2 * step]
                high, low = halves(value)
                sent[by - 1][start : start + step] = high.astype(BF16)
                sent[by - 1][start + step : start + 2 * step] = low.astype(BF16)


def lower_body(lines, share, hidden_share, own_ref, *refs):
    *got, proj_ref, mat_ref, unit_ref, swap_ref = refs
    total = own_ref[...]
    for ref in got:
        total = total + ref[...].astype(F32)
    base = hidden_share + share
    proj_ref[...] = total[:hidden_share]
    mat_ref[...] = total[hidden_share:base]
    unit_ref[...] = total[base : base + 1] + total[base + 1 : base + 2]
    for j in range(lines):
        start = base + 8 + j * share
        swap_ref[j] = total[start : start + share].astype(BF16)


def upper_body(lines, share, part, own_ref, *refs):
    *got, swap_ref, high_ref, low_ref = refs
    total = own_ref[...]
    for ref in got:
        total = total + ref[...].astype(F32)
    base = lines * share
    value = total[base : base + 16] + total[base + 16 : base + 32]
    high, low = halves(value)
    high_ref[...] = jnp.zeros_like(high_ref)
    low_ref[...] = jnp.zeros_like(low_ref)
    for j in range(lines):
        for source, target in ((high, high_ref), (low, low_ref)):
            for v in range(5):
                at, lane = 2 * v + j * part // (2 * part), (j % 2) * part
                target[v : v + 1, :part] = source[at : at + 1, lane : lane + part]
            target[5:6] = source[10:11]
        swap_ref[j, 0:8] = high_ref[...].astype(BF16)
        swap_ref[j, 8:16] = low_ref[...].astype(BF16)
        swap_ref[j, 16:] = total[j * share : (j + 1) * share].astype(BF16)


def land_body(part, got_ref, out_ref, sums_ref, row_ref):
    lines = got_ref.shape[0]
    third = lines * part
    sums = jnp.zeros((8, part), F32)
    for j in range(lines):
        value = got_ref[j, 0:8].astype(F32) + got_ref[j, 8:16].astype(F32)
        sums = sums + value[:, :part]
        for kind in range(3):
            source = slice(kind * part, (kind + 1) * part)
            target = slice(kind * third + j * part, kind * third + (j + 1) * part)
            out_ref[:, target] = got_ref[j, 16:, source].astype(F32)
            row_ref[:, target] = value[5:6, source]
    sums_ref[...] = sums


def attend_back_body(own, heads, grad_ref, qkv_ref, prev_ref, probs_ref, context_ref, mat_ref,
                     d_own_ref, d_prev_ref, d_context_ref):
    part = heads * HEAD
    scale = HEAD ** (-0.5)

    @pl.loop(0, qkv_ref.shape[0])
    def _(i):
        d_context_ref[...] = times(grad_ref[i], mat_ref[...], (1, 1)).astype(BF16)
        for head in range(heads):
            start = head * HEAD
            lanes = slice(start, start + HEAD)
            keys = both_halves(prev_ref, qkv_ref, i, part + start)
            values = both_halves(prev_ref, qkv_ref, i, 2 * part + start)
            d_context = d_context_ref[:, lanes]
            row_dot = jnp.sum(
                d_context.astype(F32) * context_ref[i, :, lanes].astype(F32), -1, keepdims=True
            )
            weights = probs_ref[i, head]
            d_scores = weights * (times(d_context, values, (1, 1)) - row_dot) * scale
            d_scores = d_scores.astype(BF16)
            d_keys = times(d_scores, qkv_ref[i, :, lanes], (0, 0))
            d_values = times(weights.astype(BF16), d_context, (0, 0))
            d_own_ref[i, :, lanes] = times(d_scores, keys, (1, 0))
            d_own_ref[i, :, part + start : part + start + HEAD] = d_keys[own:]
            d_own_ref[i, :, 2 * part + start : 2 * part + start + HEAD] = d_values[own:]
            d_prev_ref[i, :, lanes] = d_keys[:own].astype(BF16)
            d_prev_ref[i, :, part + start : part + start + HEAD] = d_values[:own].astype(BF16)


def project_back_body(own, part, lines, dims, place_ref, sums2_ref, d_own_ref, back_ref, cos_ref, sine_ref, acts1_ref, weights_ref,
                      vectors_ref, normed_ref, e_ref, first_ref, *rest):
    pieces, rest = rest[: lines - 1], rest[lines - 1 :]
    if dims:
        kept_ref, given_ref, grad_ref, sums_ref, column_ref, whole_ref, d_ref, extra_ref = rest
    else:
        grad_ref, sums_ref, column_ref, whole_ref, d_ref = rest
    whole_ref[...] = d_own_ref[...]
    whole_ref[:, part:] += back_ref[...].astype(F32)
    for start in range(0, 2 * part, LANES):
        lanes = slice(start, start + LANES)
        whole_ref[:, lanes] = turned(whole_ref[:, lanes], cos_ref[...], -sine_ref[...])
    column_ref[0:1] = jnp.sum(whole_ref[...], 0, keepdims=True)
    d_ref[...] = whole_ref[...].astype(BF16)
    d_acts1 = times(d_ref[...], weights_ref[:, : 3 * part], (1, 1))
    sums_ref[0:1] = jnp.sum(d_acts1 * normed_ref[...], 0, keepdims=True)
    sums_ref[1:2] = jnp.sum(d_acts1, 0, keepdims=True)
    total = d_acts1 * vectors_ref[0:1] + e_ref[...]
    first_ref[...] = total[:own]
    for i, piece in enumerate(pieces):
        piece[...] = total[(i + 1) * own : (i + 2) * own].astype(BF16)
    grad_ref[...] = times(acts1_ref[...], d_ref[...], (0, 0))
    if dims:
        ranks, share = dims
        core = place_ref[0]
        extra_ref[...] = jnp.zeros_like(extra_ref)
        wide = 2 * part
        vectors = (sums_ref[0:1], sums_ref[1:2], sums2_ref[0:1], sums2_ref[1:2], sums2_ref[2:3])
        for v, vector in enumerate(vectors):
            extra_ref[2 * v : 2 * v + 1, :wide] = vector[:, :wide]
            extra_ref[2 * v + 1 : 2 * v + 2, :wide] = vector[:, wide:]
        extra_ref[10:11] = column_ref[0:1]
        high, low = halves(extra_ref[...])
        base = lines * share
        for i in range(ranks):
            for j in range(lines):
                dealt(core, grad_ref, kept_ref, given_ref, i, j * share,
                      (j * ranks + i) * 2 * share, share)
            kept_ref[i, base : base + 16] = extra_ref[...]
            kept_ref[i, base + 16 : base + 32] = jnp.zeros_like(high)
            given_ref[i, base : base + 16] = high.astype(BF16)
            given_ref[i, base + 16 : base + 32] = low.astype(BF16)


def finish_body(count, x_ref, grad_ref, first_ref, *rest):
    total = first_ref[...]
    for i in range(count):
        total = total + rest[i][...].astype(F32)
    x = x_ref[...].astype(F32)
    centred = x - jnp.mean(x, -1, keepdims=True)
    inverse = lax.rsqrt(jnp.mean(centred * centred, -1, keepdims=True) + EPSILON)
    normed = centred * inverse
    rest[count][...] = (
        grad_ref[...].astype(F32)
        + inverse
        * (
            total
            - jnp.mean(total, -1, keepdims=True)
            - normed * jnp.mean(total * normed, -1, keepdims=True)
        )
    ).astype(BF16)


def two_parts(values):
    high = lax.reduce_precision(values, 8, 7)
    return jnp.concatenate([high, lax.reduce_precision(values - high, 8, 7)], -1)


def joined(row, size):
    return row[..., :size] + row[..., size : 2 * size]


def padded(values, width):
    return jnp.pad(values, [(0, 0)] * (values.ndim - 1) + [(0, width - values.shape[-1])])


def local(
    block_in,
    doc_ids,
    positions,
    ln1_gain,
    ln1_bias,
    qkv_weight,
    qkv_bias,
    attn_weight,
    attn_bias,
    ln2_gain,
    ln2_bias,
    fc_weight,
    fc_bias,
    proj_weight,
    proj_bias,
    grad_out,
):
    lines, ranks, cores = (lax.axis_size(axis) for axis in ("m", "r", "c"))
    row_count, local_len, width = block_in.shape
    own = row_count * local_len
    tokens = lines * own
    heads = HEADS // lines
    part = heads * HEAD
    share = qkv_weight.shape[0]
    hidden_share = proj_weight.shape[0]
    units = fc_weight.shape[1] // lines
    third = qkv_weight.shape[1] // 3
    columns = 3 * part + units

    vectors = [ln1_gain, ln1_bias, ln2_gain, ln2_bias, attn_bias, proj_bias, qkv_bias, fc_bias]
    length = sum(v.shape[0] for v in vectors)
    count = length // share
    length = -(-length // LANES) * LANES
    small, start = jnp.zeros((1, length), BF16), 0
    for v in vectors:
        end = start + v.shape[0]
        small = small + jnp.pad(v[None], ((0, 0), (start, length - end)))
        start = end
    packed = kernel_call(
        functools.partial(pack_body, lines, part, units, count),
        (shape(lines, share, columns + LANES, dtype=BF16),),
        0,
    )(qkv_weight, fc_weight, small)[0]
    packed = exchange(packed, "m")
    lower = jnp.concatenate([proj_weight, attn_weight], 0)
    split = ((0, hidden_share), (hidden_share, share))
    where = jnp.stack([lax.axis_index("c"), lax.axis_index("r")]).astype(jnp.int32)
    fast = ranks <= MOST and share % 8 == 0 and lines == 4
    if not fast:
        lower = in_order(*around(lower))
        proj_mat = lower[:, :, :hidden_share].reshape(units, width)
        out_mat = lower[:, :, hidden_share:].reshape(part, width)
        weights = in_order(*around(packed)).transpose(2, 0, 1, 3, 4)
    else:

        def ordered(split, outs, mine, other):
            return kernel_call(
                functools.partial(order_body, ranks, split), outs, 0, scalars=1
            )(where, *mine, *other)

        proj_mat, out_mat = ordered(
            split, (shape(units, width, dtype=BF16), shape(part, width, dtype=BF16)), *around(lower)
        )
        weights = ordered(
            ((0, share),),
            (shape(lines, width // lines, columns + LANES, dtype=BF16),),
            *around(packed),
        )[0]
    weights = weights.reshape(width, columns + LANES)
    line = lax.axis_index("m")
    spot = jnp.arange(3 * part)
    spot = (spot // part) * third + line * part + spot % part
    per = qkv_bias.shape[0]
    at_q = ((spot // per) * share + spot % share)[None]
    row_q = ((spot % per) // share)[None]
    spot = line * units + jnp.arange(units)
    per = fc_bias.shape[0]
    at_f = ((spot // per) * share + spot % share)[None]
    row_f = ((spot % per) // share)[None]
    frequency = 10000.0 ** (-(jnp.arange(ROT // 2).astype(F32) * 2.0 / ROT))
    frequency = jnp.broadcast_to(frequency[:, None], (ROT // 2, own))

    own_in = block_in.reshape(own, width)
    own_grad = grad_out.reshape(own, width)
    place = padded(positions.reshape(1, own).astype(BF16), width)
    sent = jnp.concatenate([own_in, jnp.broadcast_to(place, (8, width))], 0)
    arrived = [sent] + [shifted(sent, "m", by) for by in range(1, lines)]
    late_grad = after(own_grad, weights)
    grads = [own_grad] + [shifted(late_grad, "m", by) for by in range(1, lines)]

    def project(*refs):
        project_body(own, part, lines, refs[:lines], refs[lines:])

    qkv, acts1, acts2, normed, cosine, sine, place, vectors = kernel_call(
        project,
        (
            shape(tokens, 3 * part, dtype=BF16),
            shape(tokens, width, dtype=BF16),
            shape(tokens, width, dtype=BF16),
            shape(tokens, width),
            shape(tokens, LANES),
            shape(tokens, LANES),
            shape(tokens, LANES),
            shape(8, width),
        ),
        2 * tokens * width * 3 * part,
    )(*arrived, weights, at_q, row_q, at_f, row_f, frequency)
    qkv = qkv.reshape(lines, own, 3 * part)
    prev = lax.ppermute(qkv, "c", [(i, i + 1) for i in range(cores - 1)])
    hidden, slope, mlp_out = kernel_call(
        functools.partial(hidden_body, part),
        (shape(tokens, units, dtype=BF16), shape(tokens, units), shape(tokens, width)),
        4 * tokens * width * units,
    )(acts2, weights, proj_mat, vectors)
    probs, context, first, *outward = kernel_call(
        functools.partial(attend_body, own, heads),
        (
            shape(lines, heads, own, 2 * own),
            shape(lines, own, part, dtype=BF16),
            shape(own, width),
            *[shape(own, width, dtype=BF16)] * (lines - 1),
        ),
        8 * tokens * own * part,
        [pltpu.VMEM((lines, own, width), BF16)],
    )(qkv, prev, place.reshape(lines, own, LANES), out_mat, mlp_out.reshape(lines, own, width))
    block_sum = first
    for by in range(1, lines):
        block_sum = block_sum + shifted(outward[by - 1], "m", -by).astype(F32)
    block_out = (own_in.astype(F32) + block_sum + (vectors[4] + vectors[5])).astype(BF16)

    grads = after(tuple(grads), first)
    base = hidden_share + share + 8
    plain = (
        shape(units, width),
        shape(width, units),
        shape(part, width),
        shape(8, units),
    )
    dealt_rows = base + lines * share
    sums2, e_hidden, grads, *given1 = kernel_call(
        functools.partial(
            hidden_back_body, part, lines, own, (ranks, share, hidden_share) if fast else None
        ),
        (
            shape(8, width),
            shape(tokens, width),
            shape(tokens, width, dtype=BF16),
            *(
                (
                    shape(ranks, dealt_rows, width),
                    shape(ranks, dealt_rows, width, dtype=BF16),
                )
                if fast
                else plain
            ),
        ),
        8 * tokens * width * units,
        [pltpu.VMEM(a.shape, a.dtype) for a in plain] if fast else [],
        scalars=1,
    )(where, *grads, hidden, slope, acts2, weights, proj_mat, vectors, normed,
      context.reshape(tokens, part))
    if fast:
        got1 = swapped(given1[1])
    d_own, d_prev = kernel_call(
        functools.partial(attend_back_body, own, heads),
        (
            shape(lines, own, 3 * part),
            shape(lines, own, 2 * part, dtype=BF16),
        ),
        16 * tokens * own * part,
        [pltpu.VMEM((own, part), BF16)],
    )(grads.reshape(lines, own, width), qkv, prev, probs, context, out_mat)
    back = lax.ppermute(d_prev, "c", [(i + 1, i) for i in range(cores - 1)])
    if fast:
        own1, *sent1 = kernel_call(
            functools.partial(fold_body, ranks, hidden_share + share, 1),
            (
                shape(dealt_rows, width),
                *[shape(dealt_rows, width, dtype=BF16)] * (ranks - 1),
            ),
            0,
            scalars=1,
        )(where, given1[0], after(got1, back))
        got1 = [shifted(sent1[by - 1], "r", -by) for by in range(1, ranks)]
    plain = (shape(width, 3 * part), shape(8, width), shape(8, 3 * part))
    dealt_rows = lines * share + 32
    first, *rest = kernel_call(
        functools.partial(
            project_back_body, own, part, lines, (ranks, share) if fast else None
        ),
        (
            shape(own, width),
            *[shape(own, width, dtype=BF16)] * (lines - 1),
            *(
                (
                    shape(ranks, dealt_rows, 3 * part),
                    shape(ranks, dealt_rows, 3 * part, dtype=BF16),
                )
                if fast
                else plain
            ),
        ),
        4 * tokens * width * 3 * part,
        ([pltpu.VMEM(a.shape, a.dtype) for a in plain] if fast else [])
        + [pltpu.VMEM((tokens, 3 * part), F32), pltpu.VMEM((tokens, 3 * part), BF16)]
        + ([pltpu.VMEM((16, 3 * part), F32)] if fast else []),
        scalars=1,
    )(
        where, sums2, d_own.reshape(tokens, 3 * part), back.reshape(tokens, 2 * part), cosine, sine, acts1,
        weights, vectors, normed, e_hidden,
    )
    outward, given2 = rest[: lines - 1], rest[lines - 1 :]
    grad_in = kernel_call(
        functools.partial(finish_body, lines - 1), (shape(own, width, dtype=BF16),), 0
    )(own_in, own_grad, first, *[shifted(outward[by - 1], "m", -by) for by in range(1, lines)])[0]
    block_out = block_out.reshape(row_count, local_len, width)
    grad_in = grad_in.reshape(row_count, local_len, width)
    if fast:
        out_proj, out_attn, unit, swap = kernel_call(
            functools.partial(lower_body, lines, share, hidden_share),
            (
                shape(hidden_share, width),
                shape(share, width),
                shape(1, units),
                shape(lines, share, units, dtype=BF16),
            ),
            0,
        )(own1, *got1)
        rank, core = lax.axis_index("r"), lax.axis_index("c")
        spot = rank * cores + core
        out_fc_vec = lax.dynamic_slice_in_dim(unit[0], spot * hidden_share, hidden_share, 0)
        swap = exchange(swap, "m")
        out_fc = swap.transpose(1, 0, 2).reshape(share, lines * units).astype(F32)
        got2 = swapped(given2[1])
        own2, *sent2 = kernel_call(
            functools.partial(fold_body, ranks, lines * share, 16),
            (
                shape(dealt_rows, 3 * part),
                *[shape(dealt_rows, 3 * part, dtype=BF16)] * (ranks - 1),
            ),
            0,
            scalars=1,
        )(where, given2[0], got2)
        got2 = [shifted(sent2[by - 1], "r", -by) for by in range(1, ranks)]
        swap = kernel_call(
            functools.partial(upper_body, lines, share, part),
            (shape(lines, 16 + share, 3 * part, dtype=BF16),),
            0,
            [pltpu.VMEM((8, 3 * part), F32), pltpu.VMEM((8, 3 * part), F32)],
        )(own2, *got2)[0]
        out_qkv, sums, row = kernel_call(
            functools.partial(land_body, part),
            (shape(share, 3 * third), shape(8, part), shape(1, 3 * third)),
            0,
        )(exchange(swap, "m"))
        sums = lax.dynamic_slice_in_dim(sums, spot * share, share, 1)
        per = qkv_bias.shape[0]
        spot = (line * ranks + rank) * cores + core
        out_qkv_vec = lax.dynamic_slice_in_dim(row[0], spot * per, per, 0)
        return (
            block_out, grad_in, sums[0], sums[1], out_qkv, out_qkv_vec, out_attn, sums[4],
            sums[2], sums[3], out_fc, out_fc_vec, out_proj, sums[4],
        )

    grad_proj, grad_fc, grad_attn, unit_sums = given1
    grad_qkv, sums1, columns_sum = given2
    grad_fc_vec, grad_qkv_vec = unit_sums[0], columns_sum[0]
    grad_gain1, grad_bias1, grad_gain2, grad_bias2 = sums1[0], sums1[1], sums2[0], sums2[1]
    grad_sum = sums2[2]

    lower = pair_summed(
        jnp.concatenate(
            [
                grad_attn.reshape(ranks, cores, share, width),
                grad_proj.reshape(ranks, cores, hidden_share, width),
                padded(two_parts(grad_fc_vec.reshape(ranks, cores, 1, hidden_share)), width),
            ],
            2,
        ),
        1,
    )
    lower = jnp.concatenate(
        [lower[:, :-1], padded(two_parts(joined(lower[:, -1:], hidden_share)), width)], 1
    )
    lower = summed(lower.astype(BF16), "r")
    out_attn = lower[:share]
    out_proj = lower[share:-1]
    out_fc_vec = joined(lower[-1], hidden_share)

    upper = pair_summed(grad_fc.reshape(lines, ranks, cores, share, units), 2)
    upper = summed(upper.astype(BF16).transpose(1, 0, 2, 3), "r")
    upper = exchange(upper.astype(BF16), "m")
    out_fc = upper.transpose(1, 0, 2).reshape(share, lines * units).astype(F32)

    spots = jnp.zeros((3, third), F32)
    spots = lax.dynamic_update_slice(spots, grad_qkv_vec.reshape(3, part), (0, line * part))
    extras = jnp.concatenate(
        [
            vector.reshape(lines, ranks, cores, -1)
            for vector in (grad_gain1, grad_bias1, grad_gain2, grad_bias2, grad_sum, spots)
        ],
        -1,
    )[:, :, :, None]
    size = extras.shape[-1]
    upper = jnp.concatenate(
        [
            grad_qkv.reshape(lines, ranks, cores, share, 3 * part),
            padded(two_parts(extras), 3 * part),
        ],
        3,
    )

    def repacked(sums):
        return jnp.concatenate(
            [sums[..., :share, :], padded(two_parts(joined(sums[..., share:, :], size)), 3 * part)],
            -2,
        ).astype(BF16)

    upper = repacked(pair_summed(upper, 2)).transpose(1, 0, 2, 3)
    upper = exchange(repacked(summed(upper, "r")), "m").astype(F32)
    out_qkv = upper[:, :share].reshape(lines, share, 3, part).transpose(1, 2, 0, 3)
    out_qkv = out_qkv.reshape(share, 3 * third)
    extras = jnp.sum(joined(upper[:, share], size), 0)
    out_gain1, out_bias1, out_gain2, out_bias2, out_sum = (
        extras[i * share : (i + 1) * share] for i in range(5)
    )
    out_qkv_vec = extras[5 * share :]
    return (
        block_out,
        grad_in,
        out_gain1,
        out_bias1,
        out_qkv,
        out_qkv_vec,
        out_attn,
        out_sum,
        out_gain2,
        out_bias2,
        out_fc,
        out_fc_vec,
        out_proj,
        out_sum,
    )


def solution(mesh):
    lines = math.gcd(HEADS, mesh.shape["dp"])
    grid = Mesh(
        mesh.devices.reshape(lines, mesh.shape["dp"] // lines, mesh.shape["seq"]), ("m", "r", "c")
    )
    rows = P(("m", "r"), "c", None)
    marks = P(("m", "r"), "c")
    vector = P(("m", "r", "c"))
    matrix = P(("m", "r", "c"), None)

    return jax.shard_map(
        local,
        mesh=grid,
        in_specs=(
            rows, marks, marks, vector, vector, matrix, vector, matrix, vector,
            vector, vector, matrix, vector, matrix, vector, rows,
        ),
        out_specs=(
            rows, rows, vector, vector, matrix, vector, matrix, vector,
            vector, vector, matrix, vector, matrix, vector,
        ),
        check_vma=False,
    )
```

time: 780 us -> 197 us (0.25)
  waiting for transfers between devices: 605 us -> 37.2 us
  blocking collectives: 82.2 us -> 15.9 us
  Pallas kernels: 0 us -> 65.5 us
  matrix products: 47.1 us -> 0 us
  starting transfers between devices: 8.92 us -> 53.2 us
  between operations: 14.8 us -> 1.07 us
    reduce_scatter x4 -> x0, waiting for transfers between devices: 441 us -> none  [the longest x1 142 us: local(): lax.psum_scatter(grad_proj_weight, ('dp', 'seq'), scatter_dimension=0, ti...]
    all_gather x4 -> x0, waiting for transfers between devices: 159 us -> none  [the longest x1 59.9 us: local(): lax.all_gather(qkv_weight, ('dp', 'seq'), axis=0, tiled=True)]
    unnamed x2 -> x0, blocking collectives: 82.2 us -> none
    pallas_call x0 -> x15, Pallas kernels: none -> 65.5 us  [run(): pl.pallas_call(body, out_shape=outs, in_specs=[pl.BlockSpec(memory_space=...]
    dot_general x18 -> x0, matrix products: 47.1 us -> none  [the longest x1 7.59 us: local(): jnp.dot(acts2, fc_mat, preferred_element_type=float_type)]
    ppermute x5 -> x36, starting transfers between devices: 8.43 us -> 42.8 us  [the longest x24 37.8 us: shifted(): lax.ppermute(value, axis, [(i, (i - by) % count) for i in range(count)])]
    ppermute x5 -> x36, waiting for transfers between devices: 2.41 us -> 33.3 us  [the longest x24 30.1 us: shifted(): lax.ppermute(value, axis, [(i, (i - by) % count) for i in range(count)])]
    all_to_all x0 -> x1, blocking collectives: none -> 15.9 us  [exchange(): return lax.all_to_all(blocks, axis, 0, 0)]
  transfers between devices with their start and end apart: 13 -> 38, of which waited for: 10 -> 14; matrix products, arithmetic and copies ran while one was open for 8% -> 6% of each run, Pallas kernels for 0% -> 20%
where the time goes in v1:
time: 197 us; the launch traced here: 196 us
  Pallas kernels  65.5 us (33%)
  starting transfers between devices  53.2 us (27%)
  waiting for transfers between devices  37.2 us (19%)
  local copies, waits for them, and re-layouts  16.3 us (8%)
  blocking collectives  15.9 us (8%)
  other arithmetic  6.69 us (3%)
    pallas_call x15, Pallas kernels, run(): pl.pallas_call(body, out_shape=outs, in_specs=[pl.BlockSpec(memory_space=...  65.5 us
    ppermute x24, starting transfers between devices, shifted(): lax.ppermute(value, axis, [(i, (i - by) % count) for i in range(count)])  37.8 us
    ppermute x24, waiting for transfers between devices, shifted(): lax.ppermute(value, axis, [(i, (i - by) % count) for i in range(count)])  30.1 us
    all_to_all x1, blocking collectives, exchange(): return lax.all_to_all(blocks, axis, 0, 0)  15.9 us
    all_to_all x2, starting transfers between devices, exchange(): return lax.all_to_all(blocks, axis, 0, 0)  10.3 us
    unnamed x86, local copies, waits for them, and re-layouts  6.16 us
  transfers between devices with their start and end apart: 38, of which 14 were waited for; matrix products, arithmetic and copies ran while one was open for 6% of the time, Pallas kernels for 20%

profile of v1, /device:TPU:0, one launch (start us, length us, event | category | flops | bytes accessed | tf_op | source)
XLA Modules:
  0.0 195.9 jit_solution(15280303982946221986)
XLA Ops:
  0.7 1.5 pad_add_fusion.small_ref
  2.1 1.9 shard_map.254
  4.0 15.9 %all_to_all.15.refs_0_ = bf16[4,24,1472]{2,1,0:T(8,128)(2,1)S(1)} all-to-all(bf16[4,24,1472]{2,1,0:T(8,128)(2,1)} %shard_map.254), channel_id=1, replica_groups=mesh['m'=4,'r'=4,'c'=2] {'m'}, dimensions={0} | all-to-all | bytes 565248 | tf_op jit(solution)/shard_map/all_to_all | solution.py:30
  19.9 1.5 collective-permute-start.5
  22.1 1.6 collective-permute-start.4
  23.7 1.4 collective-permute-start.3
  26.6 4.1 %collective-permute-done.5.refs_3_ = bf16[4,24,1472]{2,1,0:T(8,128)(2,1)S(1)} collective-permute-done((bf16[4,24,1472]{2,1,0:T(8,128)(2,1)S(1)}, bf16[4,24,1472]{2,1,0:T(8,128)(2,1)S(1)}, u32[]{:S(2)}, u32[]{:S(2)}) %collective-permute-start.5) | collective-permute-done | bytes 282656 | tf_op jit(solution)/shard_map/ppermute | solution.py:26
  32.1 2.5 %collective-permute-done.4.refs_2_ = bf16[4,24,1472]{2,1,0:T(8,128)(2,1)S(1)} collective-permute-done((bf16[4,24,1472]{2,1,0:T(8,128)(2,1)S(1)}, bf16[4,24,1472]{2,1,0:T(8,128)(2,1)S(1)}, u32[]{:S(2)}, u32[]{:S(2)}) %collective-permute-start.4) | collective-permute-done | bytes 282656 | tf_op jit(solution)/shard_map/ppermute | solution.py:26
  35.1 1.3 collective-permute-start.1
  39.7 3.5 %shard_map.255 = bf16[4,192,1472]{2,1,0:T(8,128)(2,1)} custom-call(s32[2]{0:T(128)} %pad_add_fusion.1.place_ref.refs_0_, bf16[4,24,1472]{2,1,0:T(8,128)(2,1)} %copy-done.2, bf16[4,24,1472]{2,1,0:T(8,128)(2,1)} %copy-done.14, bf16[4,24,1472]{2,1,0:T(8,128)(2,1)} %copy-done.13, bf16[4,24,1472]{2,1,0:T(8,128)(2,1)} %copy-done.12, ...), custom_call_target="tpu_custom_call" | custom-call | bytes 4521992 | tf_op jit(solution)/shard_map/pallas_call | solution.py:101
  43.2 4.1 %collective-permute-done.1.refs_2_ = bf16[136,768]{1,0:T(8,128)(2,1)S(1)} collective-permute-done((bf16[136,768]{1,0:T(8,128)(2,1)S(1)}, bf16[136,768]{1,0:T(8,128)(2,1)S(1)}, u32[]{:S(2)}, u32[]{:S(2)}) %collective-permute-start.1) | collective-permute-done | bytes 208928 | tf_op jit(solution)/shard_map/ppermute | solution.py:26
  48.5 5.7 %shard_map.256 = (bf16[512,576]{1,0:T(8,128)(2,1)}, bf16[512,768]{1,0:T(8,128)(2,1)}, bf16[512,768]{1,0:T(8,128)(2,1)}, f32[512,768]{1,0:T(8,128)}, f32[512,128]...) custom-call(bf16[136,768]{1,0:T(8,128)(2,1)} %copy-done.3, bf16[136,768]{1,0:T(8,128)(2,1)} %copy-done.21, ...), custom_call_target="tpu_custom_call" | custom-call | flops 452984832 | bytes 7657984 | tf_op jit(solution)/shard_map/pallas_call | solution.py:101
  54.2 1.4 copy.30
  55.6 1.5 collective-permute-start.10
  57.1 2.6 %collective-permute-start.13 = (bf16[120,768]{1,0:T(8,128)(2,1)S(1)}, bf16[120,768]{1,0:T(8,128)(2,1)S(1)}, u32[]{:S(2)}, u32[]{:S(2)}) collective-permute-start(bf16[120,768]{1,0:T(8,128)(2,1)S(1)} %constant_dynamic-update-slice_fusion.refs_0_), channel_id=1, source_target_pairs={{0,2},{2,4},{4,6},{6,0},{1,3},{3,5},{5,7},{7,1},{8,10},{10,12},{12... | collective-permute-start | bytes 552968 | tf_op jit(solution)/shard_map/ppermute | solution.py:26
  60.2 1.4 collective-permute-start.11
  61.6 3.8 %collective-permute-done.13.refs_3_ = bf16[120,768]{1,0:T(8,128)(2,1)S(1)} collective-permute-done((bf16[120,768]{1,0:T(8,128)(2,1)S(1)}, bf16[120,768]{1,0:T(8,128)(2,1)S(1)}, u32[]{:S(2)}, u32[]{:S(2)}) %collective-permute-start.13) | collective-permute-done | bytes 184352 | tf_op jit(solution)/shard_map/ppermute | solution.py:26
  65.4 2.5 %collective-permute-done.12.refs_2_ = bf16[120,768]{1,0:T(8,128)(2,1)S(1)} collective-permute-done((bf16[120,768]{1,0:T(8,128)(2,1)S(1)}, bf16[120,768]{1,0:T(8,128)(2,1)S(1)}, u32[]{:S(2)}, u32[]{:S(2)}) %collective-permute-start.12) | collective-permute-done | bytes 184352 | tf_op jit(solution)/shard_map/ppermute | solution.py:26
  68.5 5.0 %collective-permute-start.23 = (bf16[128,768]{1,0:T(8,128)(2,1)S(1)}, bf16[128,768]{1,0:T(8,128)(2,1)S(1)}, u32[]{:S(2)}, u32[]{:S(2)}) collective-permute-start(bf16[128,768]{1,0:T(8,128)(2,1)S(1)} %bitcast.57), channel_id=1, source_target_pairs={{0,8},{8,16},{16,24},{24,0},{1,9},{9,17},{17,25},{25,1},{2,10},{10... | collective-permute-start | bytes 589832 | tf_op jit(solution)/shard_map/ppermute | solution.py:26
  73.5 2.4 %collective-permute-start.22 = (bf16[128,768]{1,0:T(8,128)(2,1)S(1)}, bf16[128,768]{1,0:T(8,128)(2,1)S(1)}, u32[]{:S(2)}, u32[]{:S(2)}) collective-permute-start(bf16[128,768]{1,0:T(8,128)(2,1)S(1)} %bitcast.58), channel_id=1, source_target_pairs={{0,16},{8,24},{16,0},{24,8},{1,17},{9,25},{17,1},{25,9},{2,18},{10... | collective-permute-start | bytes 589832 | tf_op jit(solution)/shard_map/ppermute | solution.py:26
  76.6 2.8 %shard_map.257 = (bf16[768,768]{1,0:T(8,128)(2,1)}, bf16[192,768]{1,0:T(8,128)(2,1)}) custom-call(s32[2]{0:T(128)} %pad_add_fusion.1.place_ref.refs_0_, bf16[120,768]{1,0:T(8,128)(2,1)} %copy-done.6, bf16[120,768]{1,0:T(8,128)(2,1)} %copy-done.30, bf16[120,768]{1,0:T(8,128)(2,1)} %copy-done.29, bf16[120,768]{1,0:T(8,128)(2,1)} %copy-done.28, ...), custom_call_target="tpu_custom_call" | custom-call | bytes 2949128 | tf_op jit(solution)/shard_map/pallas_call | solution.py:101
  79.5 5.5 %shard_map.258 = (bf16[512,768]{1,0:T(8,128)(2,1)}, f32[512,768]{1,0:T(8,128)}, f32[512,768]{1,0:T(8,128)}) custom-call(bf16[512,768]{1,0:T(8,128)(2,1)} %get-tuple-element.70.acts2_ref.refs_7_, bf16[768,1472]{1,0:T(8,128)(2,1)} %bitcast.43, bf16[768,768]{1,0:T(8,128)(2,1)} %get-tuple-element.71.proj_ref.refs_9_, f32[8,768]{1,0:T(8,128)} %get-tuple-element.72.vectors_ref.refs_10_), custom_call_target="tpu_custom_call" | custom-call | flops 1207959552 | bytes 8183808 | tf_op jit(solution)/shard_map/pallas_call | solution.py:101
  86.1 8.2 %shard_map.259 = (f32[4,3,128,256]{3,2,1,0:T(8,128)}, bf16[4,128,192]{2,1,0:T(8,128)(2,1)}, f32[128,768]{1,0:T(8,128)}, bf16[128,768]{1,0:T(8,128)(2,1)}, bf16[1...) custom-call(bf16[4,128,576]{2,1,0:T(8,128)(2,1)} %bitcast.47, bf16[4,128,576]{2,1,0:T(8,128)(2,1)} %copy.31.prev_ref, ...), custom_call_target="tpu_custom_call" | custom-call | flops 100663296 | bytes 6062080 | tf_op jit(solution)/shard_map/pallas_call | solution.py:101
  95.1 8.9 %shard_map.260 = (f32[8,768]{1,0:T(8,128)}, f32[512,768]{1,0:T(8,128)}, bf16[512,768]{1,0:T(8,128)(2,1)}, f32[4,224,768]{2,1,0:T(8,128)}, bf16[4,224,768]{2,1,0:T(8,128)(2,1)}) custom-call(s32[2]{0:T(128)} %pad_add_fusion.1.place_ref.refs_0_, bf16[128,768]{1,0:T(8,128)(2,1)} %bitcast.55, bf16[128,768]{1,0:T(8,128)(2,1)} %copy-done.27, ...), custom_call_target="tpu_custom_call" | custom-call | flops 2415919104 | bytes 15679496 | tf_op jit(solution)/shard_map/pallas_call | solution.py:101
  104.0 7.7 %shard_map.261 = (f32[4,128,576]{2,1,0:T(8,128)}, bf16[4,128,384]{2,1,0:T(8,128)(2,1)}) custom-call(bf16[4,128,768]{2,1,0:T(8,128)(2,1)} %bitcast.54, bf16[4,128,576]{2,1,0:T(8,128)(2,1)} %bitcast.48, bf16[4,128,576]{2,1,0:T(8,128)(2,1)} %copy.31.prev_ref, f32[4,3,128,256]{3,2,1,0:T(8,128)} %get-tuple-element.89.probs_ref, ...), custom_call_target="tpu_custom_call" | custom-call | flops 201326592 | bytes 5603328 | tf_op jit(solution)/shard_map/pallas_call | solution.py:101
  116.2 6.7 %shard_map.262 = (f32[128,768]{1,0:T(8,128)}, bf16[128,768]{1,0:T(8,128)(2,1)}, bf16[128,768]{1,0:T(8,128)(2,1)}, bf16[128,768]{1,0:T(8,128)(2,1)}, f32[4,128,57...) custom-call(s32[2]{0:T(128)} %pad_add_fusion.1.place_ref.refs_0_, f32[8,768]{1,0:T(8,128)} %get-tuple-element.87.sums2_ref, ...), custom_call_target="tpu_custom_call" | custom-call | flops 905969664 | bytes 11091976 | tf_op jit(solution)/shard_map/pallas_call | solution.py:101
  123.0 1.4 copy.33
  124.6 1.9 collective-permute-done.28
  127.6 2.4 %shard_map.264 = (f32[128,576]{1,0:T(8,128)}, bf16[128,576]{1,0:T(8,128)(2,1)}, bf16[128,576]{1,0:T(8,128)(2,1)}, bf16[128,576]{1,0:T(8,128)(2,1)}) custom-call(s32[2]{0:T(128)} %pad_add_fusion.1.place_ref.refs_0_, f32[4,128,576]{2,1,0:T(8,128)} %get-tuple-element.100.kept_ref, bf16[4,128,576]{2,1,0:T(8,128)(2,1)} %copy.34.got_ref), custom_call_target="tpu_custom_call" | custom-call | bytes 2506760 | tf_op jit(solution)/shard_map/pallas_call | solution.py:101
  130.0 1.8 collective-permute-start.29
  132.6 1.8 collective-permute-start.31
  134.4 1.4 collective-permute-start.18
  135.8 2.4 %collective-permute-done.29.refs_0_ = bf16[128,576]{1,0:T(8,128)(2,1)S(1)} collective-permute-done((bf16[128,576]{1,0:T(8,128)(2,1)}, bf16[128,576]{1,0:T(8,128)(2,1)S(1)}, u32[]{:S(2)}, u32[]{:S(2)}) %collective-permute-start.29) | collective-permute-done | bytes 147488 | tf_op jit(solution)/shard_map/ppermute | solution.py:26
  139.2 1.7 collective-permute-done.30.refs_1_
  140.8 1.4 collective-permute-start.20
  142.9 2.0 %shard_map.265 = bf16[4,40,576]{2,1,0:T(8,128)(2,1)} custom-call(f32[128,576]{1,0:T(8,128)} %get-tuple-element.102.own_ref, bf16[128,576]{1,0:T(8,128)(2,1)} %copy-done.34, bf16[128,576]{1,0:T(8,128)(2,1)} %copy-done.35, bf16[128,576]{1,0:T(8,128)(2,1)} %copy-done.36), custom_call_target="tpu_custom_call" | custom-call | bytes 921600 | tf_op jit(solution)/shard_map/pallas_call | solution.py:101
  144.9 4.4 %all-to-all-start.1 = ((bf16[4,40,576]{2,1,0:T(8,128)(2,1)}), bf16[4,40,576]{2,1,0:T(8,128)(2,1)S(1)}, u32[]{:S(2)}, u32[]{:S(2)}) async-start(bf16[4,40,576]{2,1,0:T(8,128)(2,1)} %shard_map.265), calls=%async_computation.1 | async-start | bytes 409600 | tf_op jit(solution)/shard_map/all_to_all | solution.py:30
  150.2 3.0 %collective-permute-start.26 = (bf16[128,768]{1,0:T(8,128)(2,1)}, bf16[128,768]{1,0:T(8,128)(2,1)S(1)}, u32[]{:S(2)}, u32[]{:S(2)}) collective-permute-start(bf16[128,768]{1,0:T(8,128)(2,1)} %get-tuple-element.98), channel_id=1, source_target_pairs={{0,16},{8,24},{16,0},{24,8},{1,17},{9,25},{17,1},{25,9},{2,18},{10... | collective-permute-start | bytes 589832 | tf_op jit(solution)/shard_map/ppermute | solution.py:26
  153.2 3.7 %shard_map.267 = (f32[224,768]{1,0:T(8,128)}, bf16[224,768]{1,0:T(8,128)(2,1)}, bf16[224,768]{1,0:T(8,128)(2,1)}, bf16[224,768]{1,0:T(8,128)(2,1)}) custom-call(s32[2]{0:T(128)} %pad_add_fusion.1.place_ref.refs_0_, f32[4,224,768]{2,1,0:T(8,128)} %get-tuple-element.109.kept_ref, bf16[4,224,768]{2,1,0:T(8,128)(2,1)} %copy-done.1), custom_call_target="tpu_custom_call" | custom-call | bytes 5849096 | tf_op jit(solution)/shard_map/pallas_call | solution.py:101
  156.9 1.9 collective-permute-start.27
  158.8 1.8 collective-permute-start.33
  160.6 2.5 %collective-permute-start.35 = (bf16[224,768]{1,0:T(8,128)(2,1)}, bf16[224,768]{1,0:T(8,128)(2,1)S(1)}, u32[]{:S(2)}, u32[]{:S(2)}) collective-permute-start(bf16[224,768]{1,0:T(8,128)(2,1)} %get-tuple-element.115), channel_id=1, source_target_pairs={{0,6},{2,0},{4,2},{6,4},{1,7},{3,1},{5,3},{7,5},{8,14},{10,8},{12,... | collective-permute-start | bytes 1032200 | tf_op jit(solution)/shard_map/ppermute | solution.py:26
  164.0 8.3 %collective-permute-done.26.rest_1_ = bf16[128,768]{1,0:T(8,128)(2,1)S(1)} collective-permute-done((bf16[128,768]{1,0:T(8,128)(2,1)}, bf16[128,768]{1,0:T(8,128)(2,1)S(1)}, u32[]{:S(2)}, u32[]{:S(2)}) %collective-permute-start.26) | collective-permute-done | bytes 196640 | tf_op jit(solution)/shard_map/ppermute | solution.py:26
  173.1 2.5 %shard_map.263 = bf16[128,768]{1,0:T(8,128)(2,1)} custom-call(bf16[128,768]{1,0:T(8,128)(2,1)} %bitcast.50, bf16[128,768]{1,0:T(8,128)(2,1)} %bitcast.56, f32[128,768]{1,0:T(8,128)} %get-tuple-element.96.first_ref, bf16[128,768]{1,0:T(8,128)(2,1)} %copy-done.22, bf16[128,768]{1,0:T(8,128)(2,1)} %copy-done.23, bf16[128,768]{1,0:T(8,128)(2,1)} %copy-done.24), custom_call_target="tpu_custom_call" | custom-call | bytes 1572864 | tf_op jit(solution)/shard_map/pallas_call | solution.py:101
  176.2 1.7 shard_map.266
  180.2 2.2 %shard_map.268 = (f32[96,768]{1,0:T(8,128)}, f32[24,768]{1,0:T(8,128)}, f32[1,768]{1,0:T(1,128)}, bf16[4,24,768]{2,1,0:T(8,128)(2,1)}) custom-call(f32[224,768]{1,0:T(8,128)} %get-tuple-element.112.own_ref, bf16[224,768]{1,0:T(8,128)(2,1)} %copy-done.9, bf16[224,768]{1,0:T(8,128)(2,1)} %copy-done.10, bf16[224,768]{1,0:T(8,128)(2,1)} %copy-done.11), custom_call_target="tpu_custom_call" | custom-call | bytes 2239488 | tf_op jit(solution)/shard_map/pallas_call | solution.py:101
  182.4 5.9 %all-to-all-start.2 = ((bf16[4,24,768]{2,1,0:T(8,128)(2,1)}), bf16[4,24,768]{2,1,0:T(8,128)(2,1)S(1)}, u32[]{:S(2)}, u32[]{:S(2)}) async-start(bf16[4,24,768]{2,1,0:T(8,128)(2,1)} %get-tuple-element.117), calls=%async_computation.2 | async-start | bytes 294912 | tf_op jit(solution)/shard_map/all_to_all | solution.py:30
  190.7 3.9 %all-to-all-done.2 = bf16[4,24,768]{2,1,0:T(8,128)(2,1)S(1)} async-done(((bf16[4,24,768]{2,1,0:T(8,128)(2,1)}), bf16[4,24,768]{2,1,0:T(8,128)(2,1)S(1)}, u32[]{:S(2)}, u32[]{:S(2)}) %all-to-all-start.2) | async-done | bytes 147488 | tf_op jit(solution)/shard_map/all_to_all | solution.py:30
  (153 shorter events, 29.2 us)
Async XLA Ops:
  0.6 37.6 %copy-start.37 = (bf16[96,768]{1,0:T(8,128)(2,1)S(1)}, bf16[96,768]{1,0:T(8,128)(2,1)}, u32[]{:S(2)}) copy-start(bf16[96,768]{1,0:T(8,128)(2,1)} %param.28) | copy-start | bytes 442372
  19.9 18.3 %copy-start.2 = (bf16[4,24,1472]{2,1,0:T(8,128)(2,1)}, bf16[4,24,1472]{2,1,0:T(8,128)(2,1)S(1)}, u32[]{:S(2)}) copy-start(bf16[4,24,1472]{2,1,0:T(8,128)(2,1)S(1)} %all_to_all.15.refs_0_) | copy-start | bytes 847876
  19.9 10.8 %collective-permute-start.5 = (bf16[4,24,1472]{2,1,0:T(8,128)(2,1)S(1)}, bf16[4,24,1472]{2,1,0:T(8,128)(2,1)S(1)}, u32[]{:S(2)}, u32[]{:S(2)}) collective-permute-start(bf16[4,24,1472]{2,1,0:T(8,128)(2,1)S(1)} %all_to_all.15.refs_0_), channel_id=1, source_target_pairs={{0,2},{2,4},{4,6},{6,0},{1,3},{3,5},{5,7},{7,1},{8,10},{10,12},{12... | collective-permute-start | bytes 847880 | tf_op jit(solution)/shard_map/ppermute | solution.py:26
  22.1 12.5 %collective-permute-start.4 = (bf16[4,24,1472]{2,1,0:T(8,128)(2,1)S(1)}, bf16[4,24,1472]{2,1,0:T(8,128)(2,1)S(1)}, u32[]{:S(2)}, u32[]{:S(2)}) collective-permute-start(bf16[4,24,1472]{2,1,0:T(8,128)(2,1)S(1)} %all_to_all.15.refs_0_), channel_id=1, source_target_pairs={{0,4},{2,6},{4,0},{6,2},{1,5},{3,7},{5,1},{7,3},{8,12},{10,14},{12... | collective-permute-start | bytes 847880 | tf_op jit(solution)/shard_map/ppermute | solution.py:26
  23.7 11.0 %collective-permute-start.3 = (bf16[4,24,1472]{2,1,0:T(8,128)(2,1)S(1)}, bf16[4,24,1472]{2,1,0:T(8,128)(2,1)S(1)}, u32[]{:S(2)}, u32[]{:S(2)}) collective-permute-start(bf16[4,24,1472]{2,1,0:T(8,128)(2,1)S(1)} %all_to_all.15.refs_0_), channel_id=1, source_target_pairs={{0,6},{2,0},{4,2},{6,4},{1,7},{3,1},{5,3},{7,5},{8,14},{10,8},{12,... | collective-permute-start | bytes 847880 | tf_op jit(solution)/shard_map/ppermute | solution.py:26
  26.1 17.1 %copy-start.3 = (bf16[136,768]{1,0:T(8,128)(2,1)}, bf16[136,768]{1,0:T(8,128)(2,1)S(1)}, u32[]{:S(2)}) copy-start(bf16[136,768]{1,0:T(8,128)(2,1)S(1)} %pad_maximum_fusion.refs_0_) | copy-start | bytes 626692
  26.1 17.1 %collective-permute-start.2 = (bf16[136,768]{1,0:T(8,128)(2,1)S(1)}, bf16[136,768]{1,0:T(8,128)(2,1)S(1)}, u32[]{:S(2)}, u32[]{:S(2)}) collective-permute-start(bf16[136,768]{1,0:T(8,128)(2,1)S(1)} %pad_maximum_fusion.refs_0_), channel_id=1, source_target_pairs={{0,8},{8,16},{16,24},{24,0},{1,9},{9,17},{17,25},{25,1},{2,10},{10... | collective-permute-start | bytes 626696 | tf_op jit(solution)/shard_map/ppermute | solution.py:26
  26.6 8.5 %collective-permute-start.6 = (bf16[4,24,1472]{2,1,0:T(8,128)(2,1)S(1)}, bf16[4,24,1472]{2,1,0:T(8,128)(2,1)S(1)}, u32[]{:S(2)}, u32[]{:S(2)}) collective-permute-start(bf16[4,24,1472]{2,1,0:T(8,128)(2,1)S(1)} %all_to_all.15.refs_0_), channel_id=1, source_target_pairs={{0,1},{1,0},{2,3},{3,2},{4,5},{5,4},{6,7},{7,6},{8,9},{9,8},{10,11... | collective-permute-start | bytes 847880 | tf_op jit(solution)/shard_map/ppermute | solution.py:39
  30.8 5.7 %collective-permute-start.9 = (bf16[4,24,1472]{2,1,0:T(8,128)(2,1)S(1)}, bf16[4,24,1472]{2,1,0:T(8,128)(2,1)S(1)}, u32[]{:S(2)}, u32[]{:S(2)}) collective-permute-start(bf16[4,24,1472]{2,1,0:T(8,128)(2,1)S(1)} %collective-permute-done.5.refs_3_), channel_id=1, source_target_pairs={{0,1},{1,0},{2,3},{3,2},{4,5},{5,4},{6,7},{7,6},{8,9},{9,8},{10,11... | collective-permute-start | bytes 847880 | tf_op jit(solution)/shard_map/ppermute | solution.py:39
  34.6 3.6 %collective-permute-start.8 = (bf16[4,24,1472]{2,1,0:T(8,128)(2,1)S(1)}, bf16[4,24,1472]{2,1,0:T(8,128)(2,1)S(1)}, u32[]{:S(2)}, u32[]{:S(2)}) collective-permute-start(bf16[4,24,1472]{2,1,0:T(8,128)(2,1)S(1)} %collective-permute-done.4.refs_2_), channel_id=1, source_target_pairs={{0,1},{1,0},{2,3},{3,2},{4,5},{5,4},{6,7},{7,6},{8,9},{9,8},{10,11... | collective-permute-start | bytes 847880 | tf_op jit(solution)/shard_map/ppermute | solution.py:39
  34.7 3.6 %collective-permute-start.7 = (bf16[4,24,1472]{2,1,0:T(8,128)(2,1)S(1)}, bf16[4,24,1472]{2,1,0:T(8,128)(2,1)S(1)}, u32[]{:S(2)}, u32[]{:S(2)}) collective-permute-start(bf16[4,24,1472]{2,1,0:T(8,128)(2,1)S(1)} %collective-permute-done.3.refs_1_), channel_id=1, source_target_pairs={{0,1},{1,0},{2,3},{3,2},{4,5},{5,4},{6,7},{7,6},{8,9},{9,8},{10,11... | collective-permute-start | bytes 847880 | tf_op jit(solution)/shard_map/ppermute | solution.py:39
  35.1 12.2 %collective-permute-start.1 = (bf16[136,768]{1,0:T(8,128)(2,1)S(1)}, bf16[136,768]{1,0:T(8,128)(2,1)S(1)}, u32[]{:S(2)}, u32[]{:S(2)}) collective-permute-start(bf16[136,768]{1,0:T(8,128)(2,1)S(1)} %pad_maximum_fusion.refs_0_), channel_id=1, source_target_pairs={{0,16},{8,24},{16,0},{24,8},{1,17},{9,25},{17,1},{25,9},{2,18},{10... | collective-permute-start | bytes 626696 | tf_op jit(solution)/shard_map/ppermute | solution.py:26
  36.5 11.4 %collective-permute-start = (bf16[136,768]{1,0:T(8,128)(2,1)S(1)}, bf16[136,768]{1,0:T(8,128)(2,1)S(1)}, u32[]{:S(2)}, u32[]{:S(2)}) collective-permute-start(bf16[136,768]{1,0:T(8,128)(2,1)S(1)} %pad_maximum_fusion.refs_0_), channel_id=1, source_target_pairs={{0,24},{8,0},{16,8},{24,16},{1,25},{9,1},{17,9},{25,17},{2,26},{10... | collective-permute-start | bytes 626696 | tf_op jit(solution)/shard_map/ppermute | solution.py:26
  48.5 19.9 %copy-start.5 = (bf16[1,128,768]{2,1,0:T(8,128)(2,1)S(1)}, bf16[1,128,768]{2,1,0:T(8,128)(2,1)}, u32[]{:S(2)}) copy-start(bf16[1,128,768]{2,1,0:T(8,128)(2,1)} %param.30) | copy-start | bytes 589828
  55.6 29.3 %collective-permute-start.10 = (bf16[4,128,576]{1,2,0:T(8,128)(2,1)S(1)}, bf16[4,128,576]{1,2,0:T(8,128)(2,1)S(1)}, u32[]{:S(2)}, u32[]{:S(2)}) collective-permute-start(bf16[4,128,576]{1,2,0:T(8,128)(2,1)S(1)} %copy.30), channel_id=1, source_target_pairs={{0,1},{2,3},{4,5},{6,7},{8,9},{10,11},{12,13},{14,15},{16,17},{18,... | collective-permute-start | bytes 1769480 | tf_op jit(solution)/shard_map/ppermute | solution.py:584
  57.1 19.1 %copy-start.6 = (bf16[120,768]{1,0:T(8,128)(2,1)}, bf16[120,768]{1,0:T(8,128)(2,1)S(1)}, u32[]{:S(2)}) copy-start(bf16[120,768]{1,0:T(8,128)(2,1)S(1)} %constant_dynamic-update-slice_fusion.refs_0_) | copy-start | bytes 552964
  57.1 8.3 %collective-permute-start.13 = (bf16[120,768]{1,0:T(8,128)(2,1)S(1)}, bf16[120,768]{1,0:T(8,128)(2,1)S(1)}, u32[]{:S(2)}, u32[]{:S(2)}) collective-permute-start(bf16[120,768]{1,0:T(8,128)(2,1)S(1)} %constant_dynamic-update-slice_fusion.refs_0_), channel_id=1, source_target_pairs={{0,2},{2,4},{4,6},{6,0},{1,3},{3,5},{5,7},{7,1},{8,10},{10,12},{12... | collective-permute-start | bytes 552968 | tf_op jit(solution)/shard_map/ppermute | solution.py:26
  59.7 8.2 %collective-permute-start.12 = (bf16[120,768]{1,0:T(8,128)(2,1)S(1)}, bf16[120,768]{1,0:T(8,128)(2,1)S(1)}, u32[]{:S(2)}, u32[]{:S(2)}) collective-permute-start(bf16[120,768]{1,0:T(8,128)(2,1)S(1)} %constant_dynamic-update-slice_fusion.refs_0_), channel_id=1, source_target_pairs={{0,4},{2,6},{4,0},{6,2},{1,5},{3,7},{5,1},{7,3},{8,12},{10,14},{12... | collective-permute-start | bytes 552968 | tf_op jit(solution)/shard_map/ppermute | solution.py:26
  60.2 7.8 %collective-permute-start.11 = (bf16[120,768]{1,0:T(8,128)(2,1)S(1)}, bf16[120,768]{1,0:T(8,128)(2,1)S(1)}, u32[]{:S(2)}, u32[]{:S(2)}) collective-permute-start(bf16[120,768]{1,0:T(8,128)(2,1)S(1)} %constant_dynamic-update-slice_fusion.refs_0_), channel_id=1, source_target_pairs={{0,6},{2,0},{4,2},{6,4},{1,7},{3,1},{5,3},{7,5},{8,14},{10,8},{12,... | collective-permute-start | bytes 552968 | tf_op jit(solution)/shard_map/ppermute | solution.py:26
  61.6 6.8 %collective-permute-start.14 = (bf16[120,768]{1,0:T(8,128)(2,1)S(1)}, bf16[120,768]{1,0:T(8,128)(2,1)S(1)}, u32[]{:S(2)}, u32[]{:S(2)}) collective-permute-start(bf16[120,768]{1,0:T(8,128)(2,1)S(1)} %constant_dynamic-update-slice_fusion.refs_0_), channel_id=1, source_target_pairs={{0,1},{1,0},{2,3},{3,2},{4,5},{5,4},{6,7},{7,6},{8,9},{9,8},{10,11... | collective-permute-start | bytes 552968 | tf_op jit(solution)/shard_map/ppermute | solution.py:39
  65.4 10.8 %copy-start.28 = (bf16[120,768]{1,0:T(8,128)(2,1)}, bf16[120,768]{1,0:T(8,128)(2,1)S(1)}, u32[]{:S(2)}) copy-start(bf16[120,768]{1,0:T(8,128)(2,1)S(1)} %collective-permute-done.13.refs_3_) | copy-start | bytes 552964
  65.4 8.1 %collective-permute-start.17 = (bf16[120,768]{1,0:T(8,128)(2,1)S(1)}, bf16[120,768]{1,0:T(8,128)(2,1)S(1)}, u32[]{:S(2)}, u32[]{:S(2)}) collective-permute-start(bf16[120,768]{1,0:T(8,128)(2,1)S(1)} %collective-permute-done.13.refs_3_), channel_id=1, source_target_pairs={{0,1},{1,0},{2,3},{3,2},{4,5},{5,4},{6,7},{7,6},{8,9},{9,8},{10,11... | collective-permute-start | bytes 552968 | tf_op jit(solution)/shard_map/ppermute | solution.py:39
  67.9 8.0 %collective-permute-start.16 = (bf16[120,768]{1,0:T(8,128)(2,1)S(1)}, bf16[120,768]{1,0:T(8,128)(2,1)S(1)}, u32[]{:S(2)}, u32[]{:S(2)}) collective-permute-start(bf16[120,768]{1,0:T(8,128)(2,1)S(1)} %collective-permute-done.12.refs_2_), channel_id=1, source_target_pairs={{0,1},{1,0},{2,3},{3,2},{4,5},{5,4},{6,7},{7,6},{8,9},{9,8},{10,11... | collective-permute-start | bytes 552968 | tf_op jit(solution)/shard_map/ppermute | solution.py:39
  68.0 8.2 %collective-permute-start.15 = (bf16[120,768]{1,0:T(8,128)(2,1)S(1)}, bf16[120,768]{1,0:T(8,128)(2,1)}, u32[]{:S(2)}, u32[]{:S(2)}) collective-permute-start(bf16[120,768]{1,0:T(8,128)(2,1)S(1)} %collective-permute-done.11.refs_1_), channel_id=1, source_target_pairs={{0,1},{1,0},{2,3},{3,2},{4,5},{5,4},{6,7},{7,6},{8,9},{9,8},{10,11... | collective-permute-start | bytes 552968 | tf_op jit(solution)/shard_map/ppermute | solution.py:39
  68.5 25.8 %collective-permute-start.23 = (bf16[128,768]{1,0:T(8,128)(2,1)S(1)}, bf16[128,768]{1,0:T(8,128)(2,1)S(1)}, u32[]{:S(2)}, u32[]{:S(2)}) collective-permute-start(bf16[128,768]{1,0:T(8,128)(2,1)S(1)} %bitcast.57), channel_id=1, source_target_pairs={{0,8},{8,16},{16,24},{24,0},{1,9},{9,17},{17,25},{25,1},{2,10},{10... | collective-permute-start | bytes 589832 | tf_op jit(solution)/shard_map/ppermute | solution.py:26
  73.5 20.8 %collective-permute-start.22 = (bf16[128,768]{1,0:T(8,128)(2,1)S(1)}, bf16[128,768]{1,0:T(8,128)(2,1)S(1)}, u32[]{:S(2)}, u32[]{:S(2)}) collective-permute-start(bf16[128,768]{1,0:T(8,128)(2,1)S(1)} %bitcast.58), channel_id=1, source_target_pairs={{0,16},{8,24},{16,0},{24,8},{1,17},{9,25},{17,1},{25,9},{2,18},{10... | collective-permute-start | bytes 589832 | tf_op jit(solution)/shard_map/ppermute | solution.py:26
  75.9 18.4 %collective-permute-start.21 = (bf16[128,768]{1,0:T(8,128)(2,1)S(1)}, bf16[128,768]{1,0:T(8,128)(2,1)S(1)}, u32[]{:S(2)}, u32[]{:S(2)}) collective-permute-start(bf16[128,768]{1,0:T(8,128)(2,1)S(1)} %bitcast.59), channel_id=1, source_target_pairs={{0,24},{8,0},{16,8},{24,16},{1,25},{9,1},{17,9},{25,17},{2,26},{10... | collective-permute-start | bytes 589832 | tf_op jit(solution)/shard_map/ppermute | solution.py:26
  111.7 3.8 %collective-permute-start.24 = (bf16[4,128,384]{2,1,0:T(8,128)(2,1)}, bf16[4,128,384]{2,1,0:T(8,128)(2,1)S(1)}, u32[]{:S(2)}, u32[]{:S(2)}) collective-permute-start(bf16[4,128,384]{2,1,0:T(8,128)(2,1)} %get-tuple-element.91), channel_id=1, source_target_pairs={{1,0},{3,2},{5,4},{7,6},{9,8},{11,10},{13,12},{15,14},{17,16},{19,... | collective-permute-start | bytes 1179656 | tf_op jit(solution)/shard_map/ppermute | solution.py:648
  113.0 37.2 %collective-permute-start.32 = (bf16[4,224,768]{2,1,0:T(8,128)(2,1)}, bf16[4,224,768]{2,1,0:T(8,128)(2,1)S(1)}, u32[]{:S(2)}, u32[]{:S(2)}) collective-permute-start(bf16[4,224,768]{2,1,0:T(8,128)(2,1)} %get-tuple-element.110), channel_id=1, source_target_pairs={{0,1},{1,0},{2,3},{3,2},{4,5},{5,4},{6,7},{7,6},{8,9},{9,8},{10,11... | collective-permute-start | bytes 4128776 | tf_op jit(solution)/shard_map/ppermute | solution.py:39
  124.4 13.9 %copy-start.41 = (bf16[128,768]{1,0:T(8,128)(2,1)S(1)}, bf16[128,768]{1,0:T(8,128)(2,1)}, u32[]{:S(2)}) copy-start(bf16[128,768]{1,0:T(8,128)(2,1)} %get-tuple-element.76) | copy-start | bytes 589828
  124.4 16.5 %copy-start.40 = (bf16[128,768]{1,0:T(8,128)(2,1)S(1)}, bf16[128,768]{1,0:T(8,128)(2,1)}, u32[]{:S(2)}) copy-start(bf16[128,768]{1,0:T(8,128)(2,1)} %get-tuple-element.77) | copy-start | bytes 589828
  124.4 2.1 %collective-permute-start.28 = (bf16[4,128,576]{1,2,0:T(8,128)(2,1)S(1)}, bf16[4,128,576]{1,2,0:T(8,128)(2,1)S(1)}, u32[]{:S(2)}, u32[]{:S(2)}) collective-permute-start(bf16[4,128,576]{1,2,0:T(8,128)(2,1)S(1)} %copy.33), channel_id=1, source_target_pairs={{0,1},{1,0},{2,3},{3,2},{4,5},{5,4},{6,7},{7,6},{8,9},{9,8},{10,11... | collective-permute-start | bytes 1769480 | tf_op jit(solution)/shard_map/ppermute | solution.py:39
  130.0 8.2 %collective-permute-start.29 = (bf16[128,576]{1,0:T(8,128)(2,1)}, bf16[128,576]{1,0:T(8,128)(2,1)S(1)}, u32[]{:S(2)}, u32[]{:S(2)}) collective-permute-start(bf16[128,576]{1,0:T(8,128)(2,1)} %get-tuple-element.103), channel_id=1, source_target_pairs={{0,2},{2,4},{4,6},{6,0},{1,3},{3,5},{5,7},{7,1},{8,10},{10,12},{12... | collective-permute-start | bytes 442376 | tf_op jit(solution)/shard_map/ppermute | solution.py:26
  131.8 9.1 %collective-permute-start.30 = (bf16[128,576]{1,0:T(8,128)(2,1)}, bf16[128,576]{1,0:T(8,128)(2,1)S(1)}, u32[]{:S(2)}, u32[]{:S(2)}) collective-permute-start(bf16[128,576]{1,0:T(8,128)(2,1)} %get-tuple-element.104), channel_id=1, source_target_pairs={{0,4},{2,6},{4,0},{6,2},{1,5},{3,7},{5,1},{7,3},{8,12},{10,14},{12... | collective-permute-start | bytes 442376 | tf_op jit(solution)/shard_map/ppermute | solution.py:26
  132.6 9.6 %collective-permute-start.31 = (bf16[128,576]{1,0:T(8,128)(2,1)}, bf16[128,576]{1,0:T(8,128)(2,1)S(1)}, u32[]{:S(2)}, u32[]{:S(2)}) collective-permute-start(bf16[128,576]{1,0:T(8,128)(2,1)} %get-tuple-element.105), channel_id=1, source_target_pairs={{0,6},{2,0},{4,2},{6,4},{1,7},{3,1},{5,3},{7,5},{8,14},{10,8},{12,... | collective-permute-start | bytes 442376 | tf_op jit(solution)/shard_map/ppermute | solution.py:26
  134.4 22.5 %collective-permute-start.18 = (bf16[128,768]{1,0:T(8,128)(2,1)}, bf16[128,768]{1,0:T(8,128)(2,1)S(1)}, u32[]{:S(2)}, u32[]{:S(2)}) collective-permute-start(bf16[128,768]{1,0:T(8,128)(2,1)} %get-tuple-element.75), channel_id=1, source_target_pairs={{0,8},{8,16},{16,24},{24,0},{1,9},{9,17},{17,25},{25,1},{2,10},{10... | collective-permute-start | bytes 589832 | tf_op jit(solution)/shard_map/ppermute | solution.py:26
  138.2 20.6 %collective-permute-start.19 = (bf16[128,768]{1,0:T(8,128)(2,1)S(1)}, bf16[128,768]{1,0:T(8,128)(2,1)S(1)}, u32[]{:S(2)}, u32[]{:S(2)}) collective-permute-start(bf16[128,768]{1,0:T(8,128)(2,1)S(1)} %copy-done.41), channel_id=1, source_target_pairs={{0,16},{8,24},{16,0},{24,8},{1,17},{9,25},{17,1},{25,9},{2,18},{10... | collective-permute-start | bytes 589832 | tf_op jit(solution)/shard_map/ppermute | solution.py:26
  140.8 19.7 %collective-permute-start.20 = (bf16[128,768]{1,0:T(8,128)(2,1)S(1)}, bf16[128,768]{1,0:T(8,128)(2,1)S(1)}, u32[]{:S(2)}, u32[]{:S(2)}) collective-permute-start(bf16[128,768]{1,0:T(8,128)(2,1)S(1)} %copy-done.40), channel_id=1, source_target_pairs={{0,24},{8,0},{16,8},{24,16},{1,25},{9,1},{17,9},{25,17},{2,26},{10... | collective-permute-start | bytes 589832 | tf_op jit(solution)/shard_map/ppermute | solution.py:26
  142.2 18.4 %collective-permute-start.25 = (bf16[128,768]{1,0:T(8,128)(2,1)}, bf16[128,768]{1,0:T(8,128)(2,1)S(1)}, u32[]{:S(2)}, u32[]{:S(2)}) collective-permute-start(bf16[128,768]{1,0:T(8,128)(2,1)} %get-tuple-element.97), channel_id=1, source_target_pairs={{0,8},{8,16},{16,24},{24,0},{1,9},{9,17},{17,25},{25,1},{2,10},{10... | collective-permute-start | bytes 589832 | tf_op jit(solution)/shard_map/ppermute | solution.py:26
  144.9 30.6 %all-to-all-start.1 = ((bf16[4,40,576]{2,1,0:T(8,128)(2,1)}), bf16[4,40,576]{2,1,0:T(8,128)(2,1)S(1)}, u32[]{:S(2)}, u32[]{:S(2)}) async-start(bf16[4,40,576]{2,1,0:T(8,128)(2,1)} %shard_map.265), calls=%async_computation.1 | async-start | bytes 409600 | tf_op jit(solution)/shard_map/all_to_all | solution.py:30
  150.2 22.1 %collective-permute-start.26 = (bf16[128,768]{1,0:T(8,128)(2,1)}, bf16[128,768]{1,0:T(8,128)(2,1)S(1)}, u32[]{:S(2)}, u32[]{:S(2)}) collective-permute-start(bf16[128,768]{1,0:T(8,128)(2,1)} %get-tuple-element.98), channel_id=1, source_target_pairs={{0,16},{8,24},{16,0},{24,8},{1,17},{9,25},{17,1},{25,9},{2,18},{10... | collective-permute-start | bytes 589832 | tf_op jit(solution)/shard_map/ppermute | solution.py:26
  156.9 15.5 %collective-permute-start.27 = (bf16[128,768]{1,0:T(8,128)(2,1)}, bf16[128,768]{1,0:T(8,128)(2,1)S(1)}, u32[]{:S(2)}, u32[]{:S(2)}) collective-permute-start(bf16[128,768]{1,0:T(8,128)(2,1)} %get-tuple-element.99), channel_id=1, source_target_pairs={{0,24},{8,0},{16,8},{24,16},{1,25},{9,1},{17,9},{25,17},{2,26},{10... | collective-permute-start | bytes 589832 | tf_op jit(solution)/shard_map/ppermute | solution.py:26
  158.8 20.4 %collective-permute-start.33 = (bf16[224,768]{1,0:T(8,128)(2,1)}, bf16[224,768]{1,0:T(8,128)(2,1)S(1)}, u32[]{:S(2)}, u32[]{:S(2)}) collective-permute-start(bf16[224,768]{1,0:T(8,128)(2,1)} %get-tuple-element.113), channel_id=1, source_target_pairs={{0,2},{2,4},{4,6},{6,0},{1,3},{3,5},{5,7},{7,1},{8,10},{10,12},{12... | collective-permute-start | bytes 1032200 | tf_op jit(solution)/shard_map/ppermute | solution.py:26
  160.6 18.6 %collective-permute-start.34 = (bf16[224,768]{1,0:T(8,128)(2,1)}, bf16[224,768]{1,0:T(8,128)(2,1)S(1)}, u32[]{:S(2)}, u32[]{:S(2)}) collective-permute-start(bf16[224,768]{1,0:T(8,128)(2,1)} %get-tuple-element.114), channel_id=1, source_target_pairs={{0,4},{2,6},{4,0},{6,2},{1,5},{3,7},{5,1},{7,3},{8,12},{10,14},{12... | collective-permute-start | bytes 1032200 | tf_op jit(solution)/shard_map/ppermute | solution.py:26
  160.6 11.8 %copy-start.22 = (bf16[128,768]{1,0:T(8,128)(2,1)}, bf16[128,768]{1,0:T(8,128)(2,1)S(1)}, u32[]{:S(2)}) copy-start(bf16[128,768]{1,0:T(8,128)(2,1)S(1)} %collective-permute-done.25.rest_0_) | copy-start | bytes 589828
  160.6 18.6 %collective-permute-start.35 = (bf16[224,768]{1,0:T(8,128)(2,1)}, bf16[224,768]{1,0:T(8,128)(2,1)S(1)}, u32[]{:S(2)}, u32[]{:S(2)}) collective-permute-start(bf16[224,768]{1,0:T(8,128)(2,1)} %get-tuple-element.115), channel_id=1, source_target_pairs={{0,6},{2,0},{4,2},{6,4},{1,7},{3,1},{5,3},{7,5},{8,14},{10,8},{12,... | collective-permute-start | bytes 1032200 | tf_op jit(solution)/shard_map/ppermute | solution.py:26
  179.2 16.7 %copy-start.39 = (f32[24]{0:T(128)}, f32[24]{0:T(128)S(1)}, u32[]{:S(2)}) copy-start(f32[24]{0:T(128)S(1)} %get-tuple-element.156) | copy-start | bytes 292
  182.4 12.2 %all-to-all-start.2 = ((bf16[4,24,768]{2,1,0:T(8,128)(2,1)}), bf16[4,24,768]{2,1,0:T(8,128)(2,1)S(1)}, u32[]{:S(2)}, u32[]{:S(2)}) async-start(bf16[4,24,768]{2,1,0:T(8,128)(2,1)} %get-tuple-element.117), calls=%async_computation.2 | async-start | bytes 294912 | tf_op jit(solution)/shard_map/all_to_all | solution.py:30
  (32 other events, 102.6 us)
